TPU v7x, 128 devices: a whole 4x4x4 slice. The times are simulated.
128 devices in a mesh: rows: 32 (over y, x, core), tm: 4 (over z).
Axes of the slice: x: 4, y: 4, z: 4, core: 2. Of those that a mesh axis runs over, the one named last changes fastest.
Arguments:
- snapshots: bfloat16 [524288, 512], P('rows', 'tm'), may hold values from -170 to 170, as said below
- lift: bfloat16 [512, 384], replicated, may hold values from -0.3125 to 0.3125
- adjacency: int32 [1024, 6], P(('rows', 'tm')), may hold values from -1 to 1023, as said below
- codes: int32 [1024, 6], P(('rows', 'tm')), may hold values from 0 to 3, as said below
- obstacle: int32 [1024], P(('rows', 'tm')), may hold values 0 or 1
Outputs:
- modes: float32 [524288, 512], P(('rows', 'tm'))
- rfactor: float32 [512, 512], replicated
Inputs may be any that keep to these rules, and one draw needn't show every extreme that they name: `snapshots`: custom float draw with element and snapshot scales. `adjacency`: the layer of an element is its index // 8. The -z and +z neighbours lie in the layers below and above, cyclic over 128 layers; the x and y neighbours lie in the element's own layer; -1 stands only on -y or +y faces. Neighbours are mutual: e lies beyond face f xor 1 of the element beyond its face f. Quarter turns of the neighbour's face nodes; the two codes of a shared face add up to a multiple of 4; 0 on walls.
All inputs are finite; a program needn't handle non-finite values. No bound on the sum of `obstacle` on one device may be relied on, other than what follows from the above.
Results may differ from a plain program's by a relative error of at most 0.0041.
Values may be sent and summed in bfloat16 or wider, within the bound.
A program may use at most 128 MiB of HBM per device.

v0:
```python
import math

import jax
import jax.numpy as jnp
from jax import lax
from jax.sharding import Mesh
from jax.sharding import PartitionSpec as P
from jax.experimental import pallas as pl
from jax.experimental.pallas import tpu as pltpu

ROWS = ("rows_0", "rows_1", "rows_2")
ROWS_TM = ("rows_0", "rows_1", "rows_2", "tm")


def extended(x, sides, width):
    edges = {}
    for axis, dim in sides:
        peers, length = (lax.axis_size(axis), x.shape[dim])
        up = [(i, (i + 1) % peers) for i in range(peers)]
        last = lax.slice_in_dim(x, length - width, length, axis=dim)
        leading = lax.slice_in_dim(x, 0, width, axis=dim)
        edges[dim] = (
            lax.ppermute(last, axis, up),
            lax.ppermute(leading, axis, [(b, a) for a, b in up]),
        )
    done = []
    for _, dim in sides:
        low, high = edges[dim]
        around = [(width, width) if d in done else (0, 0) for d in range(x.ndim)]
        x = jnp.concatenate([jnp.pad(low, around), x, jnp.pad(high, around)], axis=dim)
        done.append(dim)
    return x


def in_blocks(x, dim, peers):
    lengths = x.shape
    tiles = x.reshape(*lengths[:dim], peers, lengths[dim] // peers, *lengths[dim + 1 :])
    return jnp.moveaxis(tiles, dim, 0)


def sum_at_owner(x, axis, dim):
    tiles = in_blocks(x, dim, lax.axis_size(axis))
    arrived = lax.all_to_all(tiles, axis, split_axis=0, concat_axis=0, tiled=True)
    return arrived.sum(axis=0)


def sum_by_axis(x, axes, dim):
    far, near = axes
    own = sum_at_owner(in_blocks(x, dim, lax.axis_size(far)), near, dim + 1)
    return jnp.sum(lax.all_to_all(own, far, 0, 0, tiled=True), axis=0)


def rows_for(lines, peers):
    spare = -lines.shape[0] % peers
    if not spare:
        return lines
    return jnp.concatenate([lines, jnp.zeros((spare, *lines.shape[1:]), lines.dtype)])


def sent_to_all(x, axis):
    copies = jnp.broadcast_to(x, (lax.axis_size(axis), *x.shape))
    return lax.all_to_all(copies, axis, split_axis=0, concat_axis=0, tiled=True)


def laid_out(tiles, dim):
    tiles = jnp.moveaxis(tiles, 0, dim)
    lengths = tiles.shape
    return tiles.reshape(*lengths[:dim], lengths[dim] * lengths[dim + 1], *lengths[dim + 2 :])


def whole_of(x, axes, dim):
    far, near = axes
    leading = sent_to_all(x, far)
    tiles = jnp.swapaxes(sent_to_all(leading, near), 0, 1)
    return laid_out(tiles.reshape(-1, *x.shape), dim)


def sum_by_parts(x, axes):
    lines = x.reshape(-1, x.shape[-1])
    own = sum_by_axis(rows_for(lines, lax.axis_size(axes[0]) * lax.axis_size(axes[1])), axes, 0)
    whole = whole_of(own, axes, 0)
    return whole[: len(lines)].reshape(x.shape)


def face_traces(nodal_block, per_side):
    final = per_side - 1
    return jnp.stack(
        [
            nodal_block[:, 0],
            nodal_block[:, final],
            nodal_block[:, :, 0],
            nodal_block[:, :, final],
            nodal_block[:, :, :, 0],
            nodal_block[:, :, :, final],
        ],
        axis=1,
    )


def weigh_layers(
    nodal_block, adjacency, codes, obstacle, lower_five, upper_four, first_elem, elem_total, lift
):
    elements = nodal_block.shape[0]
    per_side = nodal_block.shape[1]
    columns = nodal_block.shape[-1]
    per_layer = lower_five.shape[0]
    traces = face_traces(nodal_block, per_side)
    own_offset = jnp.mod(adjacency - first_elem, elem_total)
    low_offset = jnp.mod(adjacency - first_elem + per_layer, elem_total)
    tables = (
        traces[:, 1],
        traces[:, 0],
        traces[:, 3],
        traces[:, 2],
        jnp.concatenate([lower_five, traces[:, 5]], 0),
        jnp.concatenate([traces[:, 4], upper_four], 0),
    )
    offsets = (own_offset, own_offset, own_offset, own_offset, low_offset, own_offset)
    picked = jnp.stack(
        [
            jnp.take(
                tables[face_id],
                jnp.clip(offsets[face_id][:, face_id], 0, tables[face_id].shape[0] - 1),
                axis=0,
            )
            for face_id in range(6)
        ],
        axis=1,
    ).astype(jnp.float32)
    turned = jnp.zeros_like(picked)
    for quarter in range(4):
        matches = (codes == quarter)[:, :, None, None, None]
        turned = jnp.where(matches, jnp.rot90(picked, quarter, axes=(2, 3)), turned)
    turned = jnp.where((adjacency >= 0)[:, :, None, None, None], turned, 0.0)
    face_jumps = (
        (turned - traces.astype(jnp.float32)).astype(jnp.bfloat16).reshape(elements, -1, columns)
    )
    lifted = jnp.einsum("nk,eks->ens", lift, face_jumps, preferred_element_type=jnp.float32)
    damping = 1.0 - 0.5 * obstacle.astype(jnp.float32)
    weighted = (
        damping[:, None, None] * nodal_block.reshape(elements, -1, columns).astype(jnp.float32)
        + lifted
    )
    return weighted.astype(jnp.bfloat16)


F32 = jnp.float32
BF = jnp.bfloat16
HI = lax.Precision.HIGHEST


def lanes_of(x, lane):
    return jnp.broadcast_to(x[:, lane : lane + 1], x.shape)


def row_of(x, row):
    return jnp.broadcast_to(x[row : row + 1, :], x.shape)


def factor_block(a, e):
    tiles = len(a)
    sub = lax.broadcasted_iota(jnp.int32, (8, 128), 0)
    upper, inverse = [], []
    for p in range(tiles):
        s = 8 * p
        c = [lanes_of(a[p], s + j) for j in range(8)]
        pa, pe = a[p], e[p]
        ra, re = pa, pe
        for j in range(8):
            d = row_of(c[j], j)
            inv = 1.0 / d
            scale = lax.rsqrt(d)
            here = sub == j
            m = jnp.where(here, -inv, c[j] * inv)
            qa, qe = row_of(pa, j), row_of(pe, j)
            ra = jnp.where(here, qa * scale, ra)
            re = jnp.where(here, qe * scale, re)
            pa = jnp.where(here, 0.0, pa) - m * qa
            pe = jnp.where(here, 0.0, pe) - m * qe
            for k in range(j + 1, 8):
                ck = row_of(c[k], j)
                c[k] = jnp.where(here, 0.0, c[k]) - m * ck
        upper.append(ra)
        inverse.append(re)
        qa = [row_of(pa, j) for j in range(8)]
        qe = [row_of(pe, j) for j in range(8)]
        for i in range(p + 1, tiles):
            l = [lanes_of(a[i], s + j) for j in range(8)]
            ua = [l[j] * qa[j] for j in range(8)]
            ue = [l[j] * qe[j] for j in range(8)]
            a[i] = a[i] - (((ua[0] + ua[1]) + (ua[2] + ua[3])) + ((ua[4] + ua[5]) + (ua[6] + ua[7])))
            e[i] = e[i] - (((ue[0] + ue[1]) + (ue[2] + ue[3])) + ((ue[4] + ue[5]) + (ue[6] + ue[7])))
    return upper, inverse


def chol_kernel(g_ref, w_ref, modes_ref, r_ref, work, inv_hi, inv_lo, stage, sem):
    n = g_ref.shape[0]
    blocks = n // 128
    rows = w_ref.shape[0]
    work[:, 0:n] = g_ref[...]
    work[:, n : 2 * n] = jnp.zeros((n, n), F32)
    sub = lax.broadcasted_iota(jnp.int32, (8, 128), 0)
    lane = lax.broadcasted_iota(jnp.int32, (8, 128), 1)

    def out_copy(kb):
        slot = lax.rem(kb, 2)
        return pltpu.make_async_copy(
            stage.at[slot], modes_ref.at[:, pl.ds(pl.multiple_of(kb * 128, 128), 128)], sem.at[slot]
        )

    @pl.loop(0, blocks)
    def _(kb):
        r0 = pl.multiple_of(kb * 128, 128)
        a = [work[pl.ds(pl.multiple_of(r0 + 8 * i, 8), 8), pl.ds(r0, 128)] for i in range(16)]
        e = [jnp.where(lane == sub + 8 * i, 1.0, 0.0) for i in range(16)]
        upper, inverse = factor_block(a, e)
        for i in range(16):
            work[pl.ds(pl.multiple_of(r0 + 8 * i, 8), 8), pl.ds(r0, 128)] = upper[i]
            work[pl.ds(pl.multiple_of(r0 + 8 * i, 8), 8), pl.ds(pl.multiple_of(r0 + n, 128), 128)] = inverse[i]
        own = pl.ds(r0, 128)
        linv = work[own, pl.ds(pl.multiple_of(r0 + n, 128), 128)]
        rest = pl.ds(pl.multiple_of(r0 + 128, 128), n - 128)
        work[own, rest] = jnp.dot(linv, work[own, rest], precision=HI, preferred_element_type=F32)

        @pl.loop(kb + 1, blocks)
        def _(i):
            ri = pl.multiple_of(i * 128, 128)
            left = work[own, pl.ds(ri, 128)].T
            window = pl.ds(pl.multiple_of(r0 + 128, 128), n)
            work[pl.ds(ri, 128), window] = work[pl.ds(ri, 128), window] - jnp.dot(
                left, work[own, window], precision=HI, preferred_element_type=F32
            )

        row = work[own, pl.ds(n, n)]
        hi = row.astype(BF)
        inv_hi[...] = hi
        inv_lo[...] = (row - hi.astype(F32)).astype(BF)

        @pl.when(kb >= 2)
        def _():
            out_copy(kb - 2).wait()

        slot = lax.rem(kb, 2)
        NT = (((1,), (1,)), ((), ()))

        @pl.loop(0, rows // 512)
        def _(q):
            part = pl.ds(pl.multiple_of(q * 512, 512), 512)
            x = w_ref[part, :]
            stage[slot, part, :] = lax.dot_general(
                x, inv_hi[...], NT, preferred_element_type=F32
            ) + lax.dot_general(x, inv_lo[...], NT, preferred_element_type=F32)

        out_copy(kb).start()

    out_copy(blocks - 2).wait()
    out_copy(blocks - 1).wait()
    ri = lax.broadcasted_iota(jnp.int32, (n, n), 0)
    ci = lax.broadcasted_iota(jnp.int32, (n, n), 1)
    r_ref[...] = jnp.where(ri <= ci, work[:, 0:n], 0.0)


def factor_and_modes(gram, weighted):
    n = gram.shape[0]
    rows = weighted.shape[0]
    vm = pl.BlockSpec(memory_space=pltpu.VMEM)
    return pl.pallas_call(
        chol_kernel,
        name="factor_modes",
        out_shape=(jax.ShapeDtypeStruct((rows, n), F32), jax.ShapeDtypeStruct((n, n), F32)),
        in_specs=[vm, vm],
        out_specs=(pl.BlockSpec(memory_space=pl.ANY), vm),
        scratch_shapes=[
            pltpu.VMEM((n, 2 * n), F32),
            pltpu.VMEM((128, n), BF),
            pltpu.VMEM((128, n), BF),
            pltpu.VMEM((2, rows, 128), F32),
            pltpu.SemaphoreType.DMA((2,)),
        ],
    )(gram, weighted)


def on_device(snapshots, lift, adjacency, codes, obstacle):
    tm_size = lax.axis_size("tm")
    rows_size = lax.axis_size(ROWS)
    face_nodes = lift.shape[1] // 6
    per_side = math.isqrt(face_nodes)
    node_count = lift.shape[0]
    per_layer = adjacency.shape[0]
    elem_total = per_layer * rows_size * tm_size
    regrouped = lax.all_to_all(snapshots, "tm", split_axis=0, concat_axis=1, tiled=True)
    nodal_block = regrouped.reshape(per_layer, per_side, per_side, per_side, -1)
    rim_faces = jnp.stack([nodal_block[:, :, :, 0], nodal_block[:, :, :, per_side - 1]], 0)
    padded = extended(rim_faces, ((ROWS_TM, 0),), 1)
    first_elem = lax.axis_index(ROWS_TM) * per_layer
    weighted = weigh_layers(
        nodal_block, adjacency, codes, obstacle, padded[0], padded[3], first_elem, elem_total, lift
    )
    weighted = weighted.reshape(per_layer * node_count, -1)
    row_total = elem_total * node_count
    gram_local = (
        jnp.einsum("rs,rt->st", weighted, weighted, preferred_element_type=jnp.float32) / row_total
    )
    total_gram = sum_by_parts(gram_local, (("rows_0", "rows_1"), ("rows_2", "tm")))
    return factor_and_modes(total_gram, weighted)


def solution(mesh):
    split = Mesh(
        mesh.devices.reshape(4, 4, 2, mesh.shape["tm"]), ("rows_0", "rows_1", "rows_2", "tm")
    )
    return jax.shard_map(
        on_device,
        mesh=split,
        in_specs=(P(ROWS, "tm"), P(), P(ROWS_TM, None), P(ROWS_TM, None), P(ROWS_TM)),
        out_specs=(P(ROWS_TM, None), P()),
        check_vma=False,
    )
```

profile of v0, /device:TPU:1, one launch (start us, length us, event | category | flops | bytes accessed | tf_op | source)
XLA Modules:
  0.0 301.3 jit_solution(1083129738839871155)
XLA Ops:
  0.7 6.0 %all-to-all-start = ((bf16[4,4096,128]{2,1,0:T(8,128)(2,1)}), bf16[4,4096,128]{2,1,0:T(8,128)(2,1)}, u32[]{:S(2)}, u32[]{:S(2)}) async-start(bf16[4,4096,128]{2,1,0:T(8,128)(2,1)} %bitcast.87), calls=%async_computation | async-start | bytes 8388608 | tf_op jit(solution)/shard_map/all_to_all | solution.py:291
  12.8 42.8 %all-to-all-done = bf16[4,4096,128]{2,1,0:T(8,128)(2,1)} async-done(((bf16[4,4096,128]{2,1,0:T(8,128)(2,1)}), bf16[4,4096,128]{2,1,0:T(8,128)(2,1)}, u32[]{:S(2)}, u32[]{:S(2)}) %all-to-all-start) | async-done | bytes 4194336 | tf_op jit(solution)/shard_map/all_to_all | solution.py:291
  55.6 7.6 %copy.91 = bf16[4096,4,128]{2,1,0:T(4,128)(2,1)} copy(bf16[4096,4,128]{2,0,1:T(8,128)(2,1)} %bitcast.1) | data formatting | bytes 8388608 | tf_op jit(solution)/shard_map/all_to_all | solution.py:291
  63.2 7.2 %reshape.54 = bf16[8,8,8,8,512]{4,3,2,1,0:T(8,128)(2,1)} reshape(bf16[4096,4,128]{2,1,0:T(4,128)(2,1)} %copy.91) | data formatting | bytes 8388608 | tf_op jit(solution)/shard_map/reshape | solution.py:292
  70.4 2.1 slice_bitcast_fusion
  72.5 1.4 slice_bitcast_fusion.2
  73.9 5.6 %fusion.10 = (bf16[8,8,8,1,512]{4,3,2,1,0:T(2,128)(2,1)S(1)}, bf16[8,8,8,1,512]{4,3,2,1,0:T(2,128)(2,1)S(1)}) fusion(bf16[8,8,8,8,512]{4,3,2,1,0:T(8,128)(2,1)} %reshape.54), kind=kLoop, calls=%fused_computation.80 | loop fusion | bytes 2097152 | tf_op jit(solution)/shard_map/slice | solution.py:93
  82.6 2.1 collective-permute-start.1
  84.8 1.7 copy-done.6
  86.6 1.4 gather_fusion.2
  94.5 2.8 bitcast_convert_fusion
  98.3 18.6 %copy.88 = f32[4096,4,128]{2,1,0:T(4,128)} copy(f32[4096,4,128]{2,0,1:T(8,128)S(1)} %bitcast_convert_fusion) | data formatting | bytes 16777216 | tf_op jit(solution)/shard_map/convert_element_type | solution.py:141
  116.9 10.3 %reshape.57 = f32[8,512,512]{2,1,0:T(8,128)} reshape(f32[4096,4,128]{2,1,0:T(4,128)} %copy.88) | data formatting | bytes 16777216 | tf_op jit(solution)/shard_map/convert_element_type | solution.py:141
  127.2 2.4 gather_fusion.3
  129.6 2.2 bitcast_dynamic-update-slice_fusion.2
  133.1 2.3 pad_maximum_fusion
  135.3 2.6 gather_fusion.4
  137.9 2.3 pad_maximum_fusion.1
  140.2 2.6 gather_fusion.5
  145.4 4.1 %copy.96 = f32[8,6,8,8,512]{4,2,3,0,1:T(8,128)} copy(bf16[8,6,8,8,512]{4,3,2,0,1:T(8,128)(2,1)S(1)} %bitcast_dynamic-update-slice_fusion.6) | data formatting | bytes 9437184 | tf_op jit(solution)/shard_map/convert_element_type | solution.py:129
  149.6 7.3 %rev.17 = f32[8,6,8,8,512]{4,3,2,0,1:T(8,128)} reverse(bf16[8,6,8,8,512]{4,3,2,0,1:T(8,128)(2,1)S(1)} %bitcast_dynamic-update-slice_fusion.6), dimensions={2,3} | reverse | bytes 9437184 | tf_op jit(solution)/shard_map/jit(rot90)/jit(_flip)/rev | solution.py:133
  156.9 4.2 %copy.123 = f32[8,6,8,8,512]{4,2,3,0,1:T(8,128)} copy(bf16[8,6,8,8,512]{4,3,2,0,1:T(8,128)(2,1)S(1)} %bitcast_dynamic-update-slice_fusion.6) | data formatting | bytes 9437184 | tf_op jit(solution)/shard_map/convert_element_type | solution.py:129
  161.1 11.2 %rev.16 = f32[8,6,8,8,512]{4,3,2,0,1:T(8,128)} reverse(f32[8,6,8,8,512]{4,3,2,0,1:T(8,128)} %bitcast.85), dimensions={3} | reverse | bytes 12582912 | tf_op jit(solution)/shard_map/jit(rot90)/jit(_flip)/rev | solution.py:133
  172.4 9.9 %fusion.5 = bf16[8,6,8,8,512]{4,3,2,0,1:T(8,128)(2,1)S(1)} fusion(f32[8,6,8,8,512]{4,3,2,0,1:T(8,128)} %rev.16, f32[8,6,8,8,512]{4,3,2,0,1:T(8,128)} %rev.17, bf16[8,6,8,8,512]{4,3,2,0,1:T(8,128)(2,1)} %bitcast_dynamic-update-slice_fusion.2, f32[8,6,8,8,512]{4,2,3,0,1:T(8,128)} %copy.96, pred[8,6]{0,1:T(8,128)(4,1)S(1)} %copy-done.10, ...), kind=kLoop, calls=%fused_computation.13 | loop fusion | flops 14155776 | bytes 28311792 | tf_op jit(solution)/shard_map/convert_element_type | solution.py:136
  182.9 5.8 %fusion = bf16[8,512,512]{2,1,0:T(8,128)(2,1)S(1)} fusion(f32[8,512,512]{2,1,0:T(8,128)} %reshape.57, f32[8]{0:T(128)S(1)} %copy-done.13, bf16[8,384,512]{2,1,0:T(8,128)(2,1)S(1)} %bitcast.86, bf16[512,384]{1,0:T(8,128)(2,1)S(1)} %copy-done), kind=kOutput, calls=%fused_computation.7 | convolution fusion | flops 1616904192 | bytes 16121888 | tf_op jit(solution)/shard_map/nk,eks->ens/dot_general | solution.py:138
  188.7 1.9 copy-done.1
  190.6 2.4 fusion.6
  193.4 23.1 %all_to_all.36 = f32[8,16,4,512]{3,2,1,0:T(4,128)S(1)} all-to-all(f32[8,16,4,512]{3,2,1,0:T(4,128)S(1)} %bitcast.88), channel_id=1, replica_groups=mesh['rows_0'=4,'rows_1'=4,'rows_2'=2,'tm'=4] {'rows_2','tm'}, dimensions={0} | all-to-all | bytes 2097152 | tf_op jit(solution)/shard_map/all_to_all | solution.py:43
  216.7 10.1 %all_to_all.37 = f32[16,4,512]{2,1,0:T(4,128)S(1)} all-to-all(f32[16,4,512]{2,1,0:T(4,128)S(1)} %reduce_sum.18), channel_id=1, replica_groups=mesh['rows_0'=4,'rows_1'=4,'rows_2'=2,'tm'=4] {'rows_0','rows_1'}, dimensions={0} | all-to-all | bytes 262144 | tf_op jit(solution)/shard_map/all_to_all | solution.py:50
  226.8 9.9 %all_to_all.38 = f32[16,4,512]{2,1,0:T(4,128)S(1)} all-to-all(f32[16,4,512]{2,1,0:T(4,128)S(1)} %broadcast_in_dim.72), channel_id=1, replica_groups=mesh['rows_0'=4,'rows_1'=4,'rows_2'=2,'tm'=4] {'rows_0','rows_1'}, dimensions={0} | all-to-all | bytes 262144 | tf_op jit(solution)/shard_map/all_to_all | solution.py:62
  236.9 20.7 %all_to_all.39 = f32[8,16,4,512]{3,2,1,0:T(4,128)S(1)} all-to-all(f32[8,16,4,512]{3,2,1,0:T(4,128)S(1)} %broadcast_in_dim.73), channel_id=1, replica_groups=mesh['rows_0'=4,'rows_1'=4,'rows_2'=2,'tm'=4] {'rows_2','tm'}, dimensions={0} | all-to-all | bytes 2097152 | tf_op jit(solution)/shard_map/all_to_all | solution.py:62
  259.1 42.0 %factor_modes.1 = (f32[4096,512]{1,0:T(8,128)}, f32[512,512]{1,0:T(8,128)}) custom-call(f32[512,512]{1,0:T(8,128)} %reshape_reshape.8.g_ref, bf16[4096,512]{1,0:T(8,128)(2,1)} %bitcast.84), custom_call_target="tpu_custom_call" | custom-call | tf_op jit(solution)/shard_map/factor_modes/pallas_call | solution.py:267
  (80 shorter events, 23.4 us)
Async XLA Ops:
  0.6 182.0 %copy-start = (bf16[512,384]{1,0:T(8,128)(2,1)S(1)}, bf16[512,384]{1,0:T(8,128)(2,1)}, u32[]{:S(2)}) copy-start(bf16[512,384]{1,0:T(8,128)(2,1)} %param.10) | copy-start | bytes 1179652
  0.6 6.0 %copy-start.11 = (s32[8,6]{1,0:T(8,128)S(1)}, s32[8,6]{1,0:T(8,128)}, u32[]{:S(2)}) copy-start(s32[8,6]{1,0:T(8,128)} %param.12) | copy-start | bytes 580
  0.7 6.0 %copy-start.7 = (s32[8,6]{1,0:T(8,128)S(1)}, s32[8,6]{1,0:T(8,128)}, u32[]{:S(2)}) copy-start(s32[8,6]{1,0:T(8,128)} %param.11) | copy-start | bytes 580
  0.7 10.4 %copy-start.14 = (s32[8]{0:T(128)S(1)}, s32[8]{0:T(128)}, u32[]{:S(2)}) copy-start(s32[8]{0:T(128)} %param.13) | copy-start | bytes 100
  0.7 54.9 %all-to-all-start = ((bf16[4,4096,128]{2,1,0:T(8,128)(2,1)}), bf16[4,4096,128]{2,1,0:T(8,128)(2,1)}, u32[]{:S(2)}, u32[]{:S(2)}) async-start(bf16[4,4096,128]{2,1,0:T(8,128)(2,1)} %bitcast.87), calls=%async_computation | async-start | bytes 8388608 | tf_op jit(solution)/shard_map/all_to_all | solution.py:291
  72.5 7.1 %copy-start.2 = (bf16[8,8,8,8,512]{4,3,2,1,0:T(8,128)(2,1)S(1)}, bf16[8,8,8,8,512]{4,3,2,1,0:T(8,128)(2,1)}, u32[]{:S(2)}) copy-start(bf16[8,8,8,8,512]{4,3,2,1,0:T(8,128)(2,1)} %reshape.54) | copy-start | bytes 12582916
  79.6 5.2 %copy-start.3 = (bf16[8,8,8,1,512]{4,3,2,1,0:T(2,128)(2,1)}, bf16[8,8,8,1,512]{4,3,2,1,0:T(2,128)(2,1)S(1)}, u32[]{:S(2)}) copy-start(bf16[8,8,8,1,512]{4,3,2,1,0:T(2,128)(2,1)S(1)} %get-tuple-element.10) | copy-start | bytes 1572868
  79.6 5.2 %copy-start.4 = (bf16[8,8,8,1,512]{4,3,2,1,0:T(2,128)(2,1)}, bf16[8,8,8,1,512]{4,3,2,1,0:T(2,128)(2,1)S(1)}, u32[]{:S(2)}) copy-start(bf16[8,8,8,1,512]{4,3,2,1,0:T(2,128)(2,1)S(1)} %get-tuple-element.9) | copy-start | bytes 1572868
  81.7 51.3 %collective-permute-start = (bf16[1,8,8,8,512]{4,3,2,1,0:T(8,128)(2,1)}, bf16[1,8,8,8,512]{4,3,2,1,0:T(8,128)(2,1)}, u32[]{:S(2)}, u32[]{:S(2)}) collective-permute-start(bf16[1,8,8,8,512]{4,3,2,1,0:T(8,128)(2,1)} %bitcast.82), channel_id=1, source_target_pairs={{0,1},{1,2},{2,3},{3,4},{4,5},{5,6},{6,7},{7,8},{8,9},{9,10},{10,1... | collective-permute-start | bytes 1572872 | tf_op jit(solution)/shard_map/ppermute | solution.py:23
  82.6 55.4 %collective-permute-start.1 = (bf16[1,8,8,8,512]{4,3,2,1,0:T(8,128)(2,1)}, bf16[1,8,8,8,512]{4,3,2,1,0:T(8,128)(2,1)}, u32[]{:S(2)}, u32[]{:S(2)}) collective-permute-start(bf16[1,8,8,8,512]{4,3,2,1,0:T(8,128)(2,1)} %bitcast.72.clone.2), channel_id=1, source_target_pairs={{1,0},{2,1},{3,2},{4,3},{5,4},{6,5},{7,6},{8,7},{9,8},{10,9},{11,1... | collective-permute-start | bytes 1572872 | tf_op jit(solution)/shard_map/ppermute | solution.py:24
  84.8 1.7 copy-start.6
  94.5 2.8 copy-start.5
  135.3 8.8 %copy-start.12 = (pred[8]{0:T(512)(128)(4,1)S(1)}, pred[8]{0:T(512)(128)(4,1)}, u32[]{:S(2)}) copy-start(pred[8]{0:T(512)(128)(4,1)} %get-tuple-element.29) | copy-start | bytes 28
  161.1 11.2 %copy-start.8 = (pred[8,6]{0,1:T(8,128)(4,1)S(1)}, pred[8,6]{0,1:T(8,128)(4,1)}, u32[]{:S(2)}) copy-start(pred[8,6]{0,1:T(8,128)(4,1)} %copy.90) | copy-start | bytes 148
  161.1 11.2 %copy-start.9 = (pred[8,6]{0,1:T(8,128)(4,1)S(1)}, pred[8,6]{0,1:T(8,128)(4,1)}, u32[]{:S(2)}) copy-start(pred[8,6]{0,1:T(8,128)(4,1)} %copy.97) | copy-start | bytes 148
  161.1 11.2 %copy-start.10 = (pred[8,6]{0,1:T(8,128)(4,1)S(1)}, pred[8,6]{0,1:T(8,128)(4,1)}, u32[]{:S(2)}) copy-start(pred[8,6]{0,1:T(8,128)(4,1)} %copy.100) | copy-start | bytes 148
  182.2 0.6 copy-start.13
  188.7 1.9 copy-start.1
where the time goes:
time: 303 us; the launch traced here: 301 us
  local copies, waits for them, and re-layouts  106 us (35%)
  blocking collectives  63.8 us (21%)
  waiting for transfers between devices  42.8 us (14%)
  Pallas kernels  42 us (14%)
  other arithmetic  28.4 us (9%)
  starting transfers between devices  8.94 us (3%)
  matrix products  8.14 us (3%)
    all_to_all x1, waiting for transfers between devices, on_device(): lax.all_to_all(snapshots, 'tm', split_axis=0, concat_axis=1, tiled=True)  42.8 us
    pallas_call x1, Pallas kernels, factor_and_modes(): pl.pallas_call(chol_kernel, name='factor_modes', out_shape=(jax.ShapeDtyp...  42 us
    all_to_all x2, blocking collectives, sent_to_all(): return lax.all_to_all(copies, axis, split_axis=0, concat_axis=0, tiled=True)  30.7 us
    convert_element_type x2, local copies, waits for them, and re-layouts, weigh_layers(): nodal_block.reshape(elements, -1, columns).astype(jnp.float32)  28.9 us
    all_to_all x1, blocking collectives, sum_at_owner(): lax.all_to_all(tiles, axis, split_axis=0, concat_axis=0, tiled=True)  23.1 us
    rev x2, local copies, waits for them, and re-layouts, weigh_layers(): turned = jnp.where(matches, jnp.rot90(picked, quarter, axes=(2, 3)), turned)  18.6 us
    gather x6, local copies, waits for them, and re-layouts, weigh_layers(): jnp.take(tables[face_id], jnp.clip(offsets[face_id][:, face_id], 0, table...  11.8 us
    all_to_all x1, blocking collectives, sum_by_axis(): return jnp.sum(lax.all_to_all(own, far, 0, 0, tiled=True), axis=0)  10.1 us
  transfers between devices with their start and end apart: 3, of which 1 were waited for; matrix products, arithmetic and copies ran while one was open for 19% of the time, Pallas kernels for 0%

commit v1 on v0

v1 whole, which is shorter than its diff:
```python
import jax
import jax.numpy as jnp
from jax import lax
from jax.experimental import pallas as pl
from jax.experimental.pallas import tpu as pltpu
from jax.sharding import Mesh
from jax.sharding import PartitionSpec as P

ROWS = ("rows_0", "rows_1", "rows_2")
ROWS_TM = ("rows_0", "rows_1", "rows_2", "tm")
HI = lax.Precision.HIGHEST
F32 = jnp.float32
BF = jnp.bfloat16
MESH = pl.DeviceIdType.MESH
NODES = 512
LAYER = 8 * NODES
PAIR = 2 * NODES
TILES = 1280


def at(start, size, step=8):
    return pl.ds(pl.multiple_of(start, step), size)


def halves(face):
    last = face % 2
    if face < 2:
        return last * 448, 8, 1
    if face < 4:
        return last * 56, 64, 1
    return last * 7, 64, 8


def strided(ref, start, step):
    return ref[pl.ds(start, 8), :] if step == 1 else ref[pl.ds(start, 8, stride=step), :]


def weigh_kernel(
    snap_ref, lift_ref, tab_ref, out_ref, gram_ref,
    raw, nodes, sent, whole, tabs, smem_tabs, up_face, down_face, low_halo, high_halo,
    jump, gram, part, core_in, plane_in, z_in,
    load_sem, out_sem, tab_send, tab_recv, smem_sem, halo_send, halo_recv,
    send_sem, recv_sem, own_sem, core_send, core_recv, plane_send, plane_recv,
    z_send, z_recv, back_send, back_recv, pair_send, pair_recv,
):
    y, x, c, t = (lax.axis_index(n) for n in ("rows_0", "rows_1", "rows_2", "tm"))
    r = (y * 4 + x) * 2 + c
    xy = y * 4 + x

    def group(index):
        index = lax.rem(index + 32, 32)
        return (index // 8, lax.rem(index // 2, 4), lax.rem(index, 2), t)

    def plane(index):
        index = lax.rem(index, 16)
        return (index // 4, lax.rem(index, 4), c, t)

    def column(index):
        return (y, x, c, index)

    partner = (y, x, 1 - c, t)
    other = (lambda: group(r + jnp.where(c == 1, 1, -1)))

    def remote(src, dst, send, recv, device):
        return pltpu.make_async_remote_copy(
            src_ref=src, dst_ref=dst, send_sem=send, recv_sem=recv, device_id=device, device_id_type=MESH
        )

    barrier = pltpu.get_barrier_semaphore()
    for o in range(1, 4):
        pl.semaphore_signal(barrier, inc=1, device_id=column(lax.rem(t + o, 4)), device_id_type=MESH)
    pl.semaphore_signal(barrier, inc=1, device_id=partner, device_id_type=MESH)
    pl.semaphore_signal(barrier, inc=1, device_id=other(), device_id_type=MESH)

    @pl.loop(1, 16)
    def _(o):
        pl.semaphore_signal(barrier, inc=1, device_id=plane(xy + o), device_id_type=MESH)

    def load(l):
        rows = at(l * LAYER, LAYER)
        return pltpu.make_async_copy(snap_ref.at[rows, :], raw.at[rows, :], load_sem.at[l])

    for l in (3, 0, 1, 2):
        load(l).start()
    for l in (3, 0, 1, 2):
        load(l).wait()

        @pl.loop(0, LAYER // 128)
        def _(i):
            nodes[at((l + 1) * LAYER + i * 128, 128), :] = raw[at(l * LAYER + i * 128, 128), :].astype(F32)

        if l in (3, 0):
            face, buffer = (7, up_face) if l == 3 else (0, down_face)

            @pl.loop(0, 32)
            def _(i):
                base = (l + 1) * LAYER + i * 128 + face
                two = [nodes[pl.ds(base + 64 * h, 8, stride=8), :] for h in range(2)]
                buffer[at(i * 16, 16, 16), :] = jnp.concatenate(two, axis=0).astype(BF)

    pl.semaphore_wait(barrier, 20)

    def tab_copy(o):
        return remote(tab_ref, tabs.at[t], tab_send.at[o - 1], tab_recv.at[t], column(lax.rem(t + o, 4)))

    for o in range(1, 4):
        tab_copy(o).start()
    up = remote(up_face, low_halo, halo_send.at[0], halo_recv.at[0], group(r + 1))
    down = remote(down_face, high_halo, halo_send.at[1], halo_recv.at[1], group(r - 1))
    up.start()
    down.start()
    mine = pltpu.make_async_copy(tab_ref, tabs.at[t], own_sem.at[4])
    mine.start()
    mine.wait()
    for o in range(1, 4):
        src = lax.rem(t + o, 4)
        remote(tab_ref, tabs.at[src], tab_send.at[o - 1], tab_recv.at[src], column(src)).wait_recv()
    to_smem = pltpu.make_async_copy(tabs, smem_tabs, smem_sem)
    to_smem.start()
    to_smem.wait()

    sub = lax.broadcasted_iota(jnp.int32, (8, 128), 0)

    def split_step(s):
        m = lax.rem(s, 4)
        return s // 4, jnp.where(m == 3, 3, lax.rem(m + 1, 3))

    def layer_copy(q, l):
        return remote(
            sent.at[at(l * LAYER + q * PAIR, PAIR), :],
            whole.at[at(q * PAIR, PAIR), at(t * 128, 128, 128)],
            send_sem.at[l, q], recv_sem.at[t, q], column(l),
        )

    def own_copy(q):
        return pltpu.make_async_copy(
            sent.at[at(t * LAYER + q * PAIR, PAIR), :],
            whole.at[at(q * PAIR, PAIR), at(t * 128, 128, 128)], own_sem.at[q],
        )

    def send_step(s):
        q, l = split_step(s)

        @pl.when(l == t)
        def _():
            own_copy(q).start()

        @pl.when(l != t)
        def _():
            layer_copy(q, l).start()

    @pl.loop(0, 16)
    def _(s):
        q, l = split_step(s)
        slot = lax.rem(s, 2)

        @pl.when(s == 2)
        def _():
            for copy, halo, layer, face in ((up, low_halo, 0, 7), (down, high_halo, 5, 0)):
                copy.wait_recv()

                @pl.loop(0, 32)
                def _(i):
                    two = halo[at(i * 16, 16, 16), :].astype(F32)
                    base = layer * LAYER + i * 128 + face
                    nodes[pl.ds(base, 8, stride=8), :] = two[0:8]
                    nodes[pl.ds(base + 64, 8, stride=8), :] = two[8:16]

        for h in range(2):
            e = 2 * q + h
            own = ((l + 1) * 8 + e) * NODES
            for f in range(6):
                n = smem_tabs[l, e, f]
                k = smem_tabs[l, e, 6 + f]
                shift = (0, 0, 0, 0, -1, 1)[f]
                base = ((l + 1 + shift) * 8 + (n & 7)) * NODES
                turn = jnp.where((k == 1) | (k == 2), 1, 0)
                odd = (k & 1) == 1
                order = jnp.where(k >= 2, 7 - sub, sub)
                wall = n < 0
                nb_first, nb_tile, nb_sub = halves(f ^ 1)
                my_first, my_tile, my_sub = halves(f)
                done = []
                for i in range(8):
                    j = i + turn * (7 - 2 * i)
                    straight = strided(nodes, base + nb_first + j * nb_tile, nb_sub)
                    across = strided(nodes, base + nb_first + j * nb_sub, nb_tile)
                    got = jnp.where(odd, across, straight)
                    got = jnp.take_along_axis(got, order, axis=0)
                    got = jnp.where(wall, 0.0, got)
                    done.append(got - strided(nodes, own + my_first + i * my_tile, my_sub))
                for i in range(4):
                    two = jnp.concatenate(done[2 * i : 2 * i + 2], axis=0).astype(BF)
                    jump[slot, f * 64 + 16 * i : f * 64 + 16 * i + 16, h * 128 : h * 128 + 128] = two

        damp = [1.0 - 0.5 * smem_tabs[l, 2 * q + h, 12].astype(F32) for h in range(2)]
        for m in range(4):
            lifted = jnp.dot(
                lift_ref[m * 128 : m * 128 + 128, :], jump[slot], preferred_element_type=F32
            )
            for h in range(2):
                e = 2 * q + h
                here = nodes[at(((l + 1) * 8 + e) * NODES + m * 128, 128), :]
                sent[at((l * 8 + e) * NODES + m * 128, 128), :] = (
                    damp[h] * here + lifted[:, h * 128 : h * 128 + 128]
                ).astype(BF)

        @pl.when(s > 0)
        def _():
            send_step(s - 1)

    send_step(15)

    TN = (((0,), (0,)), ((), ()))

    def out_copy(q):
        rows = at(q * PAIR, PAIR)
        return pltpu.make_async_copy(whole.at[rows, :], out_ref.at[rows, :], out_sem.at[q])

    gram[...] = jnp.zeros_like(gram)

    @pl.loop(0, 4)
    def _(q):
        own_copy(q).wait()

        @pl.loop(1, 4)
        def _(o):
            src = lax.rem(t + o, 4)
            remote(
                sent.at[at(q * PAIR, PAIR), :],
                whole.at[at(q * PAIR, PAIR), at(src * 128, 128, 128)],
                send_sem.at[src, q], recv_sem.at[src, q], column(src),
            ).wait_recv()

        out_copy(q).start()
        rows = at(q * PAIR, PAIR)
        v = whole[rows, :]
        for b in range(2):
            left = v[:, b * 256 : b * 256 + 256]
            gram[b * 256 : b * 256 + 256, b * 256 : 512] += lax.dot_general(
                left, v[:, b * 256 : 512], TN, preferred_element_type=F32
            )

    scale = 1.0 / (1024 * NODES)
    index = 0
    for bi in range(4):
        for bj in range(bi, 4):
            part[index * 128 : index * 128 + 128, :] = (
                gram[bi * 128 : bi * 128 + 128, bj * 128 : bj * 128 + 128] * scale
            )
            index += 1

    HALF, PART = TILES // 2, TILES // 32
    keep, give = c * HALF, (1 - c) * HALF
    core = remote(part.at[at(give, HALF), :], core_in, core_send, core_recv, partner)
    core.start()
    core.wait_recv()
    part[at(keep, HALF), :] = part[at(keep, HALF), :] + core_in[...]

    def to_owner(o):
        p = lax.rem(xy + o, 16)
        return remote(
            part.at[at(keep + p * PART, PART), :], plane_in.at[xy], plane_send.at[p], plane_recv.at[xy], plane(xy + o)
        )

    def from_peer(o):
        p = lax.rem(xy + o, 16)
        return remote(
            part.at[at(keep, PART), :], plane_in.at[p], plane_send.at[p], plane_recv.at[p], plane(xy + o)
        )

    @pl.loop(1, 16)
    def _(o):
        to_owner(o).start()

    plane_in[xy] = part[at(keep + xy * PART, PART), :]

    @pl.loop(1, 16)
    def _(o):
        from_peer(o).wait_recv()

    total = plane_in[0]
    for p in range(1, 16):
        total = total + plane_in[p]
    z_in[t] = total

    def to_column(o):
        dst = lax.rem(t + o, 4)
        return remote(z_in.at[t], z_in.at[t], z_send.at[o - 1], z_recv.at[t], column(dst))

    for o in range(1, 4):
        to_column(o).start()
    for o in range(1, 4):
        src = lax.rem(t + o, 4)
        remote(z_in.at[src], z_in.at[src], z_send.at[o - 1], z_recv.at[src], column(src)).wait_recv()

    def own_rows(p):
        return gram_ref.at[at(keep + p * PART, PART), :]

    def back(o):
        return remote(own_rows(xy), own_rows(xy), back_send.at[o], back_recv.at[xy], plane(xy + o))

    def back_from(o):
        p = lax.rem(xy + o, 16)
        return remote(own_rows(p), own_rows(p), back_send.at[o], back_recv.at[p], plane(xy + o))

    def across_core(p):
        return remote(own_rows(p), own_rows(p), pair_send.at[p], pair_recv.at[p], partner)

    def across_core_in(p):
        rows = gram_ref.at[at(give + p * PART, PART), :]
        return remote(rows, rows, pair_send.at[p], pair_recv.at[p], partner)

    gram_ref[at(keep + xy * PART, PART), :] = (z_in[0] + z_in[1]) + (z_in[2] + z_in[3])

    @pl.loop(1, 16)
    def _(o):
        back(o).start()

    across_core(xy).start()

    @pl.loop(1, 16)
    def _(o):
        back_from(o).wait_recv()
        across_core(lax.rem(xy + o, 16)).start()

    @pl.loop(0, 16)
    def _(p):
        across_core_in(p).wait_recv()

    for o in range(1, 4):
        tab_copy(o).wait_send()
        to_column(o).wait_send()
    up.wait_send()
    down.wait_send()
    core.wait_send()

    @pl.loop(0, 16)
    def _(s):
        q, l = split_step(s)

        @pl.when(l != t)
        def _():
            layer_copy(q, l).wait_send()

    @pl.loop(1, 16)
    def _(o):
        to_owner(o).wait_send()
        back(o).wait_send()

    @pl.loop(0, 16)
    def _(p):
        across_core(p).wait_send()

    @pl.loop(0, 4)
    def _(q):
        out_copy(q).wait()


def weigh_and_gram(snapshots, lift, table):
    vm = pl.BlockSpec(memory_space=pltpu.VMEM)
    anyspace = pl.BlockSpec(memory_space=pl.ANY)
    D = pltpu.SemaphoreType.DMA
    V = pltpu.VMEM
    return pl.pallas_call(
        weigh_kernel,
        name="weigh_gram",
        out_shape=(jax.ShapeDtypeStruct((LAYER, 512), BF), jax.ShapeDtypeStruct((TILES, 128), F32)),
        in_specs=[anyspace, vm, vm],
        out_specs=(anyspace, vm),
        scratch_shapes=[
            V((4 * LAYER, 128), BF), V((6 * LAYER, 128), F32), V((4 * LAYER, 128), BF), V((LAYER, 512), BF),
            V((4, 8, 128), jnp.int32), pltpu.SMEM((4, 8, 128), jnp.int32),
            V((NODES, 128), BF), V((NODES, 128), BF), V((NODES, 128), BF), V((NODES, 128), BF),
            V((2, 384, 256), BF), V((512, 512), F32), V((TILES, 128), F32), V((TILES // 2, 128), F32),
            V((16, TILES // 32, 128), F32), V((4, TILES // 32, 128), F32),
            D((4,)), D((4,)), D((3,)), D((4,)), D(()), D((2,)), D((2,)),
            D((4, 4)), D((4, 4)), D((5,)), D(()), D(()), D((16,)), D((16,)),
            D((3,)), D((4,)), D((16,)), D((16,)), D((16,)), D((16,)),
        ],
        compiler_params=pltpu.CompilerParams(collective_id=0, has_side_effects=True),
    )(snapshots, lift, table)


def lanes_of(x, lane):
    return jnp.broadcast_to(x[:, lane : lane + 1], x.shape)


def row_of(x, row):
    return jnp.broadcast_to(x[row : row + 1, :], x.shape)


def factor_block(a, e):
    tiles = len(a)
    sub = lax.broadcasted_iota(jnp.int32, (8, 128), 0)
    upper, inverse = [], []
    for p in range(tiles):
        s = 8 * p
        c = [lanes_of(a[p], s + j) for j in range(8)]
        pa, pe = a[p], e[p]
        ra, re = pa, pe
        for j in range(8):
            d = row_of(c[j], j)
            inv = 1.0 / d
            scale = lax.rsqrt(d)
            here = sub == j
            m = jnp.where(here, -inv, c[j] * inv)
            qa, qe = row_of(pa, j), row_of(pe, j)
            ra = jnp.where(here, qa * scale, ra)
            re = jnp.where(here, qe * scale, re)
            pa = jnp.where(here, 0.0, pa) - m * qa
            pe = jnp.where(here, 0.0, pe) - m * qe
            for k in range(j + 1, 8):
                ck = row_of(c[k], j)
                c[k] = jnp.where(here, 0.0, c[k]) - m * ck
        upper.append(ra)
        inverse.append(re)
        qa = [row_of(pa, j) for j in range(8)]
        qe = [row_of(pe, j) for j in range(8)]
        for i in range(p + 1, tiles):
            l = [lanes_of(a[i], s + j) for j in range(8)]
            ua = [l[j] * qa[j] for j in range(8)]
            ue = [l[j] * qe[j] for j in range(8)]
            a[i] = a[i] - (((ua[0] + ua[1]) + (ua[2] + ua[3])) + ((ua[4] + ua[5]) + (ua[6] + ua[7])))
            e[i] = e[i] - (((ue[0] + ue[1]) + (ue[2] + ue[3])) + ((ue[4] + ue[5]) + (ue[6] + ue[7])))
    return upper, inverse


def chol_kernel(g_ref, w_ref, modes_ref, r_ref, work, inv_hi, inv_lo, stage, sem):
    n = r_ref.shape[0]
    blocks = n // 128
    rows = w_ref.shape[0]
    work[...] = jnp.zeros_like(work)
    index = 0
    for bi in range(blocks):
        for bj in range(bi, blocks):
            work[bi * 128 : bi * 128 + 128, bj * 128 : bj * 128 + 128] = g_ref[index * 128 : index * 128 + 128, :]
            index += 1
    sub = lax.broadcasted_iota(jnp.int32, (8, 128), 0)
    lane = lax.broadcasted_iota(jnp.int32, (8, 128), 1)

    def out_copy(kb):
        slot = lax.rem(kb, 2)
        return pltpu.make_async_copy(
            stage.at[slot], modes_ref.at[:, pl.ds(pl.multiple_of(kb * 128, 128), 128)], sem.at[slot]
        )

    @pl.loop(0, blocks)
    def _(kb):
        r0 = pl.multiple_of(kb * 128, 128)
        a = [work[pl.ds(pl.multiple_of(r0 + 8 * i, 8), 8), pl.ds(r0, 128)] for i in range(16)]
        e = [jnp.where(lane == sub + 8 * i, 1.0, 0.0) for i in range(16)]
        upper, inverse = factor_block(a, e)
        for i in range(16):
            work[pl.ds(pl.multiple_of(r0 + 8 * i, 8), 8), pl.ds(r0, 128)] = upper[i]
            work[pl.ds(pl.multiple_of(r0 + 8 * i, 8), 8), pl.ds(pl.multiple_of(r0 + n, 128), 128)] = inverse[i]
        own = pl.ds(r0, 128)
        linv = work[own, pl.ds(pl.multiple_of(r0 + n, 128), 128)]
        rest = pl.ds(pl.multiple_of(r0 + 128, 128), n - 128)
        work[own, rest] = jnp.dot(linv, work[own, rest], precision=HI, preferred_element_type=F32)

        @pl.loop(kb + 1, blocks)
        def _(i):
            ri = pl.multiple_of(i * 128, 128)
            left = work[own, pl.ds(ri, 128)].T
            window = pl.ds(pl.multiple_of(r0 + 128, 128), n)
            work[pl.ds(ri, 128), window] = work[pl.ds(ri, 128), window] - jnp.dot(
                left, work[own, window], precision=HI, preferred_element_type=F32
            )

        row = work[own, pl.ds(n, n)]
        hi = row.astype(BF)
        inv_hi[...] = hi
        inv_lo[...] = (row - hi.astype(F32)).astype(BF)

        @pl.when(kb >= 2)
        def _():
            out_copy(kb - 2).wait()

        slot = lax.rem(kb, 2)
        NT = (((1,), (1,)), ((), ()))

        @pl.loop(0, rows // 512)
        def _(q):
            part = pl.ds(pl.multiple_of(q * 512, 512), 512)
            x = w_ref[part, :]
            stage[slot, part, :] = lax.dot_general(
                x, inv_hi[...], NT, preferred_element_type=F32
            ) + lax.dot_general(x, inv_lo[...], NT, preferred_element_type=F32)

        out_copy(kb).start()

    out_copy(blocks - 2).wait()
    out_copy(blocks - 1).wait()
    ri = lax.broadcasted_iota(jnp.int32, (n, n), 0)
    ci = lax.broadcasted_iota(jnp.int32, (n, n), 1)
    r_ref[...] = jnp.where(ri <= ci, work[:, 0:n], 0.0)


def factor_and_modes(gram, weighted):
    rows, n = weighted.shape
    vm = pl.BlockSpec(memory_space=pltpu.VMEM)
    return pl.pallas_call(
        chol_kernel,
        name="factor_modes",
        out_shape=(jax.ShapeDtypeStruct((rows, n), F32), jax.ShapeDtypeStruct((n, n), F32)),
        in_specs=[vm, vm],
        out_specs=(pl.BlockSpec(memory_space=pl.ANY), vm),
        scratch_shapes=[
            pltpu.VMEM((n, 2 * n), F32),
            pltpu.VMEM((128, n), BF),
            pltpu.VMEM((128, n), BF),
            pltpu.VMEM((2, rows, 128), F32),
            pltpu.SemaphoreType.DMA((2,)),
        ],
    )(gram, weighted)


def on_device(snapshots, lift, adjacency, codes, obstacle):
    table = jnp.concatenate([adjacency, codes, obstacle[:, None]], axis=1)
    table = jnp.pad(table, ((0, 0), (0, 128 - table.shape[1])))
    weighted, gram = weigh_and_gram(snapshots, lift, table)
    return factor_and_modes(gram, weighted)


def solution(mesh):
    split = Mesh(
        mesh.devices.reshape(4, 4, 2, mesh.shape["tm"]), ("rows_0", "rows_1", "rows_2", "tm")
    )
    return jax.shard_map(
        on_device,
        mesh=split,
        in_specs=(P(ROWS, "tm"), P(), P(ROWS_TM, None), P(ROWS_TM, None), P(ROWS_TM)),
        out_specs=(P(ROWS_TM, None), P()),
        check_vma=False,
    )
```

time: 303 us -> 130 us (0.43)
  local copies, waits for them, and re-layouts: 106 us -> 1.33 us
  Pallas kernels: 42 us -> 127 us
  blocking collectives: 63.8 us -> 0 us
  waiting for transfers between devices: 42.8 us -> 0 us
  other arithmetic: 28.4 us -> 0.78 us
  starting transfers between devices: 8.94 us -> 0 us
  matrix products: 8.14 us -> 0 us
    pallas_call x0 -> x1, Pallas kernels: none -> 85.4 us  [weigh_and_gram(): pl.pallas_call(weigh_kernel, name='weigh_gram', out_shape=(jax.ShapeDtype...]
    all_to_all x4 -> x0, blocking collectives: 63.8 us -> none  [the longest x2 30.7 us: sent_to_all(): return lax.all_to_all(copies, axis, split_axis=0, concat_axis=0, tiled=True)]
    all_to_all x1 -> x0, waiting for transfers between devices: 42.8 us -> none  [on_device(): lax.all_to_all(snapshots, 'tm', split_axis=0, concat_axis=1, tiled=True)]
    convert_element_type x5 -> x0, local copies, waits for them, and re-layouts: 37.6 us -> none  [the longest x2 28.9 us: weigh_layers(): nodal_block.reshape(elements, -1, columns).astype(jnp.float32)]
    rev x2 -> x0, local copies, waits for them, and re-layouts: 18.6 us -> none  [weigh_layers(): turned = jnp.where(matches, jnp.rot90(picked, quarter, axes=(2, 3)), turned)]
    convert_element_type x2 -> x0, other arithmetic: 12.7 us -> none  [the longest x1 9.87 us: weigh_layers(): (turned - traces.astype(jnp.float32)).astype(jnp.bfloat16)]
    gather x6 -> x0, local copies, waits for them, and re-layouts: 11.8 us -> none  [weigh_layers(): jnp.take(tables[face_id], jnp.clip(offsets[face_id][:, face_id], 0, table...]
    dot_general x2 -> x0, matrix products: 8.14 us -> none  [the longest x1 5.79 us: weigh_layers(): jnp.einsum('nk,eks->ens', lift, face_jumps, preferred_element_type=jnp.fl...]
  transfers between devices with their start and end apart: 3 -> 0, of which waited for: 1 -> 0; matrix products, arithmetic and copies ran while one was open for 19% -> 0% of each run, Pallas kernels for 0% -> 0%
where the time goes in v1:
time: 130 us
  Pallas kernels  127 us (98%)
  local copies, waits for them, and re-layouts  1.33 us (1%)
    pallas_call x1, Pallas kernels, weigh_and_gram(): pl.pallas_call(weigh_kernel, name='weigh_gram', out_shape=(jax.ShapeDtype...  85.4 us
    pallas_call x1, Pallas kernels, factor_and_modes(): pl.pallas_call(chol_kernel, name='factor_modes', out_shape=(jax.ShapeDtyp...  41.9 us

profile of v1, /device:TPU:1, one launch (start us, length us, event | category | flops | bytes accessed | tf_op | source)
XLA Modules:
  0.0 130.1 jit_solution(11987539091952775774)
XLA Ops:
  0.6 0.7 copy.7
  1.4 0.8 pad_add_fusion
  2.1 0.6 pad.4.tab_ref
  2.7 85.4 %weigh_gram.1 = (bf16[4096,512]{1,0:T(8,128)(2,1)}, f32[1280,128]{1,0:T(8,128)}) custom-call(bf16[16384,128]{1,0:T(8,128)(2,1)} %snap_ref.1, bf16[512,384]{1,0:T(8,128)(2,1)} %lift_ref.1, s32[8,128]{1,0:T(8,128)} %pad.4.tab_ref), custom_call_target="tpu_custom_call" | custom-call | tf_op jit(solution)/shard_map/weigh_gram/pallas_call | solution.py:365
  88.1 41.9 %factor_modes.1 = (f32[4096,512]{1,0:T(8,128)}, f32[512,512]{1,0:T(8,128)}) custom-call(f32[1280,128]{1,0:T(8,128)} %get-tuple-element.4.g_ref, bf16[4096,512]{1,0:T(8,128)(2,1)} %get-tuple-element.5.w_ref), custom_call_target="tpu_custom_call" | custom-call | tf_op jit(solution)/shard_map/factor_modes/pallas_call | solution.py:503

commit v2 on v1

--- a/solution.py
+++ b/solution.py
@@ -426,10 +426,14 @@
     return upper, inverse
 
 
-def chol_kernel(g_ref, w_ref, modes_ref, r_ref, work, inv_hi, inv_lo, stage, sem):
+def chol_kernel(g_ref, w_hbm, modes_ref, r_ref, work, w_ref, first, second, stage, sem, w_sem):
     n = r_ref.shape[0]
     blocks = n // 128
     rows = w_ref.shape[0]
+    chunk = stage.shape[1]
+    half = n // 2
+    bring = pltpu.make_async_copy(w_hbm, w_ref, w_sem)
+    bring.start()
     work[...] = jnp.zeros_like(work)
     index = 0
     for bi in range(blocks):
@@ -438,12 +442,6 @@
             index += 1
     sub = lax.broadcasted_iota(jnp.int32, (8, 128), 0)
     lane = lax.broadcasted_iota(jnp.int32, (8, 128), 1)
-
-    def out_copy(kb):
-        slot = lax.rem(kb, 2)
-        return pltpu.make_async_copy(
-            stage.at[slot], modes_ref.at[:, pl.ds(pl.multiple_of(kb * 128, 128), 128)], sem.at[slot]
-        )
 
     @pl.loop(0, blocks)
     def _(kb):
@@ -468,30 +466,40 @@
                 left, work[own, window], precision=HI, preferred_element_type=F32
             )
 
-        row = work[own, pl.ds(n, n)]
-        hi = row.astype(BF)
-        inv_hi[...] = hi
-        inv_lo[...] = (row - hi.astype(F32)).astype(BF)
-
-        @pl.when(kb >= 2)
+    for part, r0, depth in ((first, 0, half), (second, half, n)):
+        row = work[r0 : r0 + half, n : n + depth]
+        high = row.astype(BF)
+        part[:, 0:depth] = high
+        part[:, depth : 2 * depth] = (row - high.astype(F32)).astype(BF)
+    bring.wait()
+    NT = (((1,), (1,)), ((), ()))
+
+    def out_copy(q):
+        slot = lax.rem(q, 2)
+        return pltpu.make_async_copy(
+            stage.at[slot], modes_ref.at[pl.ds(pl.multiple_of(q * chunk, chunk), chunk), :], sem.at[slot]
+        )
+
+    @pl.loop(0, rows // chunk)
+    def _(q):
+        slot = lax.rem(q, 2)
+
+        @pl.when(q >= 2)
         def _():
-            out_copy(kb - 2).wait()
-
-        slot = lax.rem(kb, 2)
-        NT = (((1,), (1,)), ((), ()))
-
-        @pl.loop(0, rows // 512)
-        def _(q):
-            part = pl.ds(pl.multiple_of(q * 512, 512), 512)
-            x = w_ref[part, :]
-            stage[slot, part, :] = lax.dot_general(
-                x, inv_hi[...], NT, preferred_element_type=F32
-            ) + lax.dot_general(x, inv_lo[...], NT, preferred_element_type=F32)
-
-        out_copy(kb).start()
-
-    out_copy(blocks - 2).wait()
-    out_copy(blocks - 1).wait()
+            out_copy(q - 2).wait()
+
+        x = w_ref[pl.ds(pl.multiple_of(q * chunk, chunk), chunk), :]
+        near = x[:, 0:half]
+        stage[slot, :, 0:half] = lax.dot_general(
+            jnp.concatenate([near, near], axis=1), first[...], NT, preferred_element_type=F32
+        )
+        stage[slot, :, half:n] = lax.dot_general(
+            jnp.concatenate([x, x], axis=1), second[...], NT, preferred_element_type=F32
+        )
+        out_copy(q).start()
+
+    out_copy(rows // chunk - 2).wait()
+    out_copy(rows // chunk - 1).wait()
     ri = lax.broadcasted_iota(jnp.int32, (n, n), 0)
     ci = lax.broadcasted_iota(jnp.int32, (n, n), 1)
     r_ref[...] = jnp.where(ri <= ci, work[:, 0:n], 0.0)
@@ -500,18 +508,21 @@
 def factor_and_modes(gram, weighted):
     rows, n = weighted.shape
     vm = pl.BlockSpec(memory_space=pltpu.VMEM)
+    anyspace = pl.BlockSpec(memory_space=pl.ANY)
     return pl.pallas_call(
         chol_kernel,
         name="factor_modes",
         out_shape=(jax.ShapeDtypeStruct((rows, n), F32), jax.ShapeDtypeStruct((n, n), F32)),
-        in_specs=[vm, vm],
-        out_specs=(pl.BlockSpec(memory_space=pl.ANY), vm),
+        in_specs=[vm, anyspace],
+        out_specs=(anyspace, vm),
         scratch_shapes=[
             pltpu.VMEM((n, 2 * n), F32),
-            pltpu.VMEM((128, n), BF),
-            pltpu.VMEM((128, n), BF),
-            pltpu.VMEM((2, rows, 128), F32),
+            pltpu.VMEM((rows, n), BF),
+            pltpu.VMEM((n // 2, n), BF),
+            pltpu.VMEM((n // 2, 2 * n), BF),
+            pltpu.VMEM((2, 512, n), F32),
             pltpu.SemaphoreType.DMA((2,)),
+            pltpu.SemaphoreType.DMA(()),
         ],
     )(gram, weighted)
 

time: 130 us -> 121 us (0.931)
  Pallas kernels: 127 us -> 118 us
    pallas_call x1, Pallas kernels: 41.9 us -> 32.3 us  [factor_and_modes(): pl.pallas_call(chol_kernel, name='factor_modes', out_shape=(jax.ShapeDtyp...]
where the time goes in v2:
time: 121 us; the launch traced here: 120 us
  Pallas kernels  118 us (98%)
  local copies, waits for them, and re-layouts  1.33 us (1%)
    pallas_call x1, Pallas kernels, weigh_and_gram(): pl.pallas_call(weigh_kernel, name='weigh_gram', out_shape=(jax.ShapeDtype...  85.4 us
    pallas_call x1, Pallas kernels, factor_and_modes(): pl.pallas_call(chol_kernel, name='factor_modes', out_shape=(jax.ShapeDtyp...  32.3 us

profile of v2, /device:TPU:1, one launch (start us, length us, event | category | flops | bytes accessed | tf_op | source)
XLA Modules:
  0.0 120.5 jit_solution(7358848704080718054)
XLA Ops:
  0.6 0.7 copy.7
  1.4 0.8 pad_add_fusion
  2.1 0.6 pad.4.tab_ref
  2.7 85.4 %weigh_gram.1 = (bf16[4096,512]{1,0:T(8,128)(2,1)}, f32[1280,128]{1,0:T(8,128)}) custom-call(bf16[16384,128]{1,0:T(8,128)(2,1)} %snap_ref.1, bf16[512,384]{1,0:T(8,128)(2,1)} %lift_ref.1, s32[8,128]{1,0:T(8,128)} %pad.4.tab_ref), custom_call_target="tpu_custom_call" | custom-call | tf_op jit(solution)/shard_map/weigh_gram/pallas_call | solution.py:365
  88.1 32.3 %factor_modes.1 = (f32[4096,512]{1,0:T(8,128)}, f32[512,512]{1,0:T(8,128)}) custom-call(f32[1280,128]{1,0:T(8,128)} %get-tuple-element.4.g_ref, bf16[4096,512]{1,0:T(8,128)(2,1)} %get-tuple-element.5.w_hbm), custom_call_target="tpu_custom_call" | custom-call | tf_op jit(solution)/shard_map/factor_modes/pallas_call | solution.py:512

commit v3 on v2

--- a/solution.py
+++ b/solution.py
@@ -36,8 +36,8 @@
 
 
 def weigh_kernel(
-    snap_ref, lift_ref, tab_ref, out_ref, gram_ref,
-    raw, nodes, sent, whole, tabs, smem_tabs, up_face, down_face, low_halo, high_halo,
+    snap_ref, lift_hbm, adjacency_ref, codes_ref, obstacle_ref, out_ref, gram_ref,
+    lift_ref, lift_sem, raw, nodes, sent, whole, table, tabs, words, smem_words, up_face, down_face, low_halo, high_halo,
     jump, gram, part, core_in, plane_in, z_in,
     load_sem, out_sem, tab_send, tab_recv, smem_sem, halo_send, halo_recv,
     send_sem, recv_sem, own_sem, core_send, core_recv, plane_send, plane_recv,
@@ -59,7 +59,6 @@
         return (y, x, c, index)
 
     partner = (y, x, 1 - c, t)
-    other = (lambda: group(r + jnp.where(c == 1, 1, -1)))
 
     def remote(src, dst, send, recv, device):
         return pltpu.make_async_remote_copy(
@@ -67,14 +66,17 @@
         )
 
     barrier = pltpu.get_barrier_semaphore()
+
+    @pl.loop(1, 16)
+    def _(o):
+        pl.semaphore_signal(barrier, inc=1, device_id=plane(xy + o), device_id_type=MESH)
+
     for o in range(1, 4):
         pl.semaphore_signal(barrier, inc=1, device_id=column(lax.rem(t + o, 4)), device_id_type=MESH)
     pl.semaphore_signal(barrier, inc=1, device_id=partner, device_id_type=MESH)
-    pl.semaphore_signal(barrier, inc=1, device_id=other(), device_id_type=MESH)
-
-    @pl.loop(1, 16)
-    def _(o):
-        pl.semaphore_signal(barrier, inc=1, device_id=plane(xy + o), device_id_type=MESH)
+    pl.semaphore_signal(
+        barrier, inc=1, device_id=group(r + jnp.where(c == 1, 1, -1)), device_id_type=MESH
+    )
 
     def load(l):
         rows = at(l * LAYER, LAYER)
@@ -82,102 +84,113 @@
 
     for l in (3, 0, 1, 2):
         load(l).start()
-    for l in (3, 0, 1, 2):
+    bring_lift = pltpu.make_async_copy(lift_hbm, lift_ref, lift_sem)
+    bring_lift.start()
+
+    sub = lax.broadcasted_iota(jnp.int32, (8, 128), 0)
+    blocked = jnp.zeros((8, 128), jnp.int32)
+    for i in range(8):
+        blocked = jnp.where(sub == i, obstacle_ref[i], blocked)
+    table[...] = jnp.zeros_like(table)
+    table[0, :, 0:6] = adjacency_ref[...]
+    table[1, :, 0:6] = codes_ref[...]
+    table[2] = blocked
+
+    def widen(l):
         load(l).wait()
 
-        @pl.loop(0, LAYER // 128)
+        @pl.loop(0, LAYER // 256)
         def _(i):
-            nodes[at((l + 1) * LAYER + i * 128, 128), :] = raw[at(l * LAYER + i * 128, 128), :].astype(F32)
-
-        if l in (3, 0):
-            face, buffer = (7, up_face) if l == 3 else (0, down_face)
-
-            @pl.loop(0, 32)
-            def _(i):
-                base = (l + 1) * LAYER + i * 128 + face
-                two = [nodes[pl.ds(base + 64 * h, 8, stride=8), :] for h in range(2)]
-                buffer[at(i * 16, 16, 16), :] = jnp.concatenate(two, axis=0).astype(BF)
-
-    pl.semaphore_wait(barrier, 20)
+            nodes[at((l + 1) * LAYER + i * 256, 256), :] = raw[at(l * LAYER + i * 256, 256), :].astype(F32)
+
+    def take_face(l, face, buffer):
+        @pl.loop(0, 8)
+        def _(i):
+            for h in range(4):
+                base = (l + 1) * LAYER + i * 512 + h * 128 + face
+                two = [nodes[pl.ds(base + 64 * g, 8, stride=8), :] for g in range(2)]
+                buffer[at(i * 64 + h * 16, 16, 16), :] = jnp.concatenate(two, axis=0).astype(BF)
 
     def tab_copy(o):
-        return remote(tab_ref, tabs.at[t], tab_send.at[o - 1], tab_recv.at[t], column(lax.rem(t + o, 4)))
-
-    for o in range(1, 4):
-        tab_copy(o).start()
+        return remote(table, tabs.at[t], tab_send.at[o - 1], tab_recv.at[t], column(lax.rem(t + o, 4)))
+
     up = remote(up_face, low_halo, halo_send.at[0], halo_recv.at[0], group(r + 1))
     down = remote(down_face, high_halo, halo_send.at[1], halo_recv.at[1], group(r - 1))
+    mine = pltpu.make_async_copy(table, tabs.at[t], own_sem.at[8])
+    mine.start()
+    pl.semaphore_wait(barrier, 20)
+    for o in (2, 1, 3):
+        tab_copy(o).start()
+    widen(3)
+    take_face(3, 7, up_face)
     up.start()
+    widen(0)
+    take_face(0, 0, down_face)
     down.start()
-    mine = pltpu.make_async_copy(tab_ref, tabs.at[t], own_sem.at[4])
-    mine.start()
+    widen(1)
+    widen(2)
     mine.wait()
     for o in range(1, 4):
         src = lax.rem(t + o, 4)
-        remote(tab_ref, tabs.at[src], tab_send.at[o - 1], tab_recv.at[src], column(src)).wait_recv()
-    to_smem = pltpu.make_async_copy(tabs, smem_tabs, smem_sem)
+        remote(table, tabs.at[src], tab_send.at[o - 1], tab_recv.at[src], column(src)).wait_recv()
+    lane = lax.broadcasted_iota(jnp.int32, (8, 128), 1)
+    merged = jnp.zeros((8, 128), jnp.int32)
+    for l in range(4):
+        found, code, stop = tabs[l, 0], tabs[l, 1], tabs[l, 2]
+        word = (found & 7) + 8 * code + jnp.where(found < 0, 32, 0) + 64 * stop
+        merged = merged + pltpu.roll(jnp.where(lane < 6, word, 0), 8 * l, 1)
+    words[...] = merged
+    to_smem = pltpu.make_async_copy(words, smem_words, smem_sem)
     to_smem.start()
     to_smem.wait()
 
-    sub = lax.broadcasted_iota(jnp.int32, (8, 128), 0)
-
     def split_step(s):
-        m = lax.rem(s, 4)
-        return s // 4, jnp.where(m == 3, 3, lax.rem(m + 1, 3))
-
-    def layer_copy(q, l):
+        o = lax.rem(s, 3)
+        odd = lax.rem(t, 2)
+        other = jnp.where(o == 0, 1 + odd, jnp.where(o == 1, 3 * (1 - odd), lax.rem(t + 2, 4)))
+        return jnp.where(s < 12, s // 3, s - 12), jnp.where(s < 12, other, t)
+
+    def layer_copy(e, l):
         return remote(
-            sent.at[at(l * LAYER + q * PAIR, PAIR), :],
-            whole.at[at(q * PAIR, PAIR), at(t * 128, 128, 128)],
-            send_sem.at[l, q], recv_sem.at[t, q], column(l),
-        )
-
-    def own_copy(q):
+            sent.at[at(l * LAYER + e * NODES, NODES), :],
+            whole.at[at(e * NODES, NODES), at(t * 128, 128, 128)],
+            send_sem.at[l, e], recv_sem.at[t, e], column(l),
+        )
+
+    def own_copy(e):
         return pltpu.make_async_copy(
-            sent.at[at(t * LAYER + q * PAIR, PAIR), :],
-            whole.at[at(q * PAIR, PAIR), at(t * 128, 128, 128)], own_sem.at[q],
+            sent.at[at(t * LAYER + e * NODES, NODES), :],
+            whole.at[at(e * NODES, NODES), at(t * 128, 128, 128)], own_sem.at[e],
         )
 
     def send_step(s):
         q, l = split_step(s)
 
-        @pl.when(l == t)
+        @pl.when(s >= 12)
         def _():
-            own_copy(q).start()
-
-        @pl.when(l != t)
+            for h in range(2):
+                own_copy(2 * q + h).start()
+
+        @pl.when(s < 12)
         def _():
-            layer_copy(q, l).start()
-
-    @pl.loop(0, 16)
-    def _(s):
+            for h in range(2):
+                layer_copy(2 * q + h, l).start()
+
+    def jumps_of(s, slot):
         q, l = split_step(s)
-        slot = lax.rem(s, 2)
-
-        @pl.when(s == 2)
-        def _():
-            for copy, halo, layer, face in ((up, low_halo, 0, 7), (down, high_halo, 5, 0)):
-                copy.wait_recv()
-
-                @pl.loop(0, 32)
-                def _(i):
-                    two = halo[at(i * 16, 16, 16), :].astype(F32)
-                    base = layer * LAYER + i * 128 + face
-                    nodes[pl.ds(base, 8, stride=8), :] = two[0:8]
-                    nodes[pl.ds(base + 64, 8, stride=8), :] = two[8:16]
-
         for h in range(2):
             e = 2 * q + h
             own = ((l + 1) * 8 + e) * NODES
             for f in range(6):
-                n = smem_tabs[l, e, f]
-                k = smem_tabs[l, e, 6 + f]
+                word = smem_words[e, 8 * l + f]
+                n = word & 7
+                k = (word >> 3) & 3
                 shift = (0, 0, 0, 0, -1, 1)[f]
-                base = ((l + 1 + shift) * 8 + (n & 7)) * NODES
+                base = ((l + 1 + shift) * 8 + n) * NODES
                 turn = jnp.where((k == 1) | (k == 2), 1, 0)
                 odd = (k & 1) == 1
                 order = jnp.where(k >= 2, 7 - sub, sub)
-                wall = n < 0
+                wall = (word & 32) != 0
                 nb_first, nb_tile, nb_sub = halves(f ^ 1)
                 my_first, my_tile, my_sub = halves(f)
                 done = []
@@ -193,7 +206,9 @@
                     two = jnp.concatenate(done[2 * i : 2 * i + 2], axis=0).astype(BF)
                     jump[slot, f * 64 + 16 * i : f * 64 + 16 * i + 16, h * 128 : h * 128 + 128] = two
 
-        damp = [1.0 - 0.5 * smem_tabs[l, 2 * q + h, 12].astype(F32) for h in range(2)]
+    def weigh(s, slot):
+        q, l = split_step(s)
+        damp = [1.0 - 0.5 * (smem_words[2 * q + h, 8 * l] >> 6).astype(F32) for h in range(2)]
         for m in range(4):
             lifted = jnp.dot(
                 lift_ref[m * 128 : m * 128 + 128, :], jump[slot], preferred_element_type=F32
@@ -205,36 +220,49 @@
                     damp[h] * here + lifted[:, h * 128 : h * 128 + 128]
                 ).astype(BF)
 
-        @pl.when(s > 0)
-        def _():
-            send_step(s - 1)
-
-    send_step(15)
+    jumps_of(0, 0)
+    bring_lift.wait()
+    for copy, halo, layer, face in ((up, low_halo, 0, 7), (down, high_halo, 5, 0)):
+        copy.wait_recv()
+
+        @pl.loop(0, 8)
+        def _(i):
+            for h in range(4):
+                two = halo[at(i * 64 + h * 16, 16, 16), :].astype(F32)
+                base = layer * LAYER + i * 512 + h * 128 + face
+                nodes[pl.ds(base, 8, stride=8), :] = two[0:8]
+                nodes[pl.ds(base + 64, 8, stride=8), :] = two[8:16]
+
+    @pl.loop(0, 16)
+    def _(s):
+        slot = lax.rem(s, 2)
+        weigh(s, slot)
+        jumps_of(jnp.minimum(s + 1, 15), 1 - slot)
+        send_step(s)
 
     TN = (((0,), (0,)), ((), ()))
 
-    def out_copy(q):
-        rows = at(q * PAIR, PAIR)
-        return pltpu.make_async_copy(whole.at[rows, :], out_ref.at[rows, :], out_sem.at[q])
+    def out_copy(e):
+        rows = at(e * NODES, NODES)
+        return pltpu.make_async_copy(whole.at[rows, :], out_ref.at[rows, :], out_sem.at[e])
 
     gram[...] = jnp.zeros_like(gram)
 
-    @pl.loop(0, 4)
-    def _(q):
-        own_copy(q).wait()
+    @pl.loop(0, 8)
+    def _(e):
+        own_copy(e).wait()
 
         @pl.loop(1, 4)
         def _(o):
             src = lax.rem(t + o, 4)
             remote(
-                sent.at[at(q * PAIR, PAIR), :],
-                whole.at[at(q * PAIR, PAIR), at(src * 128, 128, 128)],
-                send_sem.at[src, q], recv_sem.at[src, q], column(src),
+                sent.at[at(e * NODES, NODES), :],
+                whole.at[at(e * NODES, NODES), at(src * 128, 128, 128)],
+                send_sem.at[src, e], recv_sem.at[src, e], column(src),
             ).wait_recv()
 
-        out_copy(q).start()
-        rows = at(q * PAIR, PAIR)
-        v = whole[rows, :]
+        out_copy(e).start()
+        v = whole[at(e * NODES, NODES), :]
         for b in range(2):
             left = v[:, b * 256 : b * 256 + 256]
             gram[b * 256 : b * 256 + 256, b * 256 : 512] += lax.dot_general(
@@ -251,33 +279,42 @@
             index += 1
 
     HALF, PART = TILES // 2, TILES // 32
+    CHUNK = HALF // 4
     keep, give = c * HALF, (1 - c) * HALF
-    core = remote(part.at[at(give, HALF), :], core_in, core_send, core_recv, partner)
-    core.start()
-    core.wait_recv()
-    part[at(keep, HALF), :] = part[at(keep, HALF), :] + core_in[...]
-
-    def to_owner(o):
-        p = lax.rem(xy + o, 16)
+
+    def core(i):
+        k = lax.rem(y + i, 4)
+        rows = at(k * CHUNK, CHUNK)
         return remote(
-            part.at[at(keep + p * PART, PART), :], plane_in.at[xy], plane_send.at[p], plane_recv.at[xy], plane(xy + o)
-        )
-
-    def from_peer(o):
-        p = lax.rem(xy + o, 16)
+            part.at[at(give + k * CHUNK, CHUNK), :], core_in.at[rows, :], core_send.at[k], core_recv.at[k], partner
+        )
+
+    def to_owner(p):
         return remote(
-            part.at[at(keep, PART), :], plane_in.at[p], plane_send.at[p], plane_recv.at[p], plane(xy + o)
-        )
+            part.at[at(keep + p * PART, PART), :], plane_in.at[xy], plane_send.at[p], plane_recv.at[xy], plane(p)
+        )
+
+    def from_peer(p):
+        return remote(
+            part.at[at(keep, PART), :], plane_in.at[p], plane_send.at[p], plane_recv.at[p], plane(p)
+        )
+
+    for i in range(4):
+        core(i).start()
+
+    for i in range(4):
+        core(i).wait_recv()
+        k = lax.rem(y + i, 4)
+        mine_rows = at(keep + k * CHUNK, CHUNK)
+        part[mine_rows, :] = part[mine_rows, :] + core_in[at(k * CHUNK, CHUNK), :]
+        for o in range(1 if i == 0 else 0, 4):
+            to_owner(k * 4 + lax.rem(x + o, 4)).start()
+
+    plane_in[xy] = part[at(keep + xy * PART, PART), :]
 
     @pl.loop(1, 16)
     def _(o):
-        to_owner(o).start()
-
-    plane_in[xy] = part[at(keep + xy * PART, PART), :]
-
-    @pl.loop(1, 16)
-    def _(o):
-        from_peer(o).wait_recv()
+        from_peer(lax.rem(xy + o, 16)).wait_recv()
 
     total = plane_in[0]
     for p in range(1, 16):
@@ -333,53 +370,57 @@
         to_column(o).wait_send()
     up.wait_send()
     down.wait_send()
-    core.wait_send()
-
-    @pl.loop(0, 16)
+    for i in range(4):
+        core(i).wait_send()
+
+    @pl.loop(0, 12)
     def _(s):
         q, l = split_step(s)
-
-        @pl.when(l != t)
-        def _():
-            layer_copy(q, l).wait_send()
+        for h in range(2):
+            layer_copy(2 * q + h, l).wait_send()
 
     @pl.loop(1, 16)
     def _(o):
-        to_owner(o).wait_send()
+        to_owner(lax.rem(xy + o, 16)).wait_send()
         back(o).wait_send()
 
     @pl.loop(0, 16)
     def _(p):
         across_core(p).wait_send()
 
-    @pl.loop(0, 4)
-    def _(q):
-        out_copy(q).wait()
-
-
-def weigh_and_gram(snapshots, lift, table):
+    @pl.loop(0, 8)
+    def _(e):
+        out_copy(e).wait()
+
+
+def weigh_and_gram(snapshots, lift, adjacency, codes, obstacle):
     vm = pl.BlockSpec(memory_space=pltpu.VMEM)
+    sm = pl.BlockSpec(memory_space=pltpu.SMEM)
     anyspace = pl.BlockSpec(memory_space=pl.ANY)
     D = pltpu.SemaphoreType.DMA
     V = pltpu.VMEM
+    I32 = jnp.int32
     return pl.pallas_call(
         weigh_kernel,
         name="weigh_gram",
         out_shape=(jax.ShapeDtypeStruct((LAYER, 512), BF), jax.ShapeDtypeStruct((TILES, 128), F32)),
-        in_specs=[anyspace, vm, vm],
+        in_specs=[anyspace, anyspace, vm, vm, sm],
         out_specs=(anyspace, vm),
         scratch_shapes=[
-            V((4 * LAYER, 128), BF), V((6 * LAYER, 128), F32), V((4 * LAYER, 128), BF), V((LAYER, 512), BF),
-            V((4, 8, 128), jnp.int32), pltpu.SMEM((4, 8, 128), jnp.int32),
+            V((NODES, 384), BF), D(()), V((4 * LAYER, 128), BF), V((6 * LAYER, 128), F32), V((4 * LAYER, 128), BF), V((LAYER, 512), BF),
+            V((3, 8, 128), I32), V((4, 3, 8, 128), I32), V((8, 128), I32), pltpu.SMEM((8, 128), I32),
             V((NODES, 128), BF), V((NODES, 128), BF), V((NODES, 128), BF), V((NODES, 128), BF),
             V((2, 384, 256), BF), V((512, 512), F32), V((TILES, 128), F32), V((TILES // 2, 128), F32),
             V((16, TILES // 32, 128), F32), V((4, TILES // 32, 128), F32),
-            D((4,)), D((4,)), D((3,)), D((4,)), D(()), D((2,)), D((2,)),
-            D((4, 4)), D((4, 4)), D((5,)), D(()), D(()), D((16,)), D((16,)),
+            D((4,)), D((8,)), D((3,)), D((4,)), D(()), D((2,)), D((2,)),
+            D((4, 8)), D((4, 8)), D((9,)), D((4,)), D((4,)), D((16,)), D((16,)),
             D((3,)), D((4,)), D((16,)), D((16,)), D((16,)), D((16,)),
         ],
         compiler_params=pltpu.CompilerParams(collective_id=0, has_side_effects=True),
-    )(snapshots, lift, table)
+    )(snapshots, lift, adjacency, codes, obstacle)
+
+
+NEAR = 2
 
 
 def lanes_of(x, lane):
@@ -390,40 +431,43 @@
     return jnp.broadcast_to(x[row : row + 1, :], x.shape)
 
 
-def factor_block(a, e):
+def factor_block(a):
     tiles = len(a)
     sub = lax.broadcasted_iota(jnp.int32, (8, 128), 0)
-    upper, inverse = [], []
+    lane = lax.broadcasted_iota(jnp.int32, (8, 128), 1)
+    rows = []
     for p in range(tiles):
         s = 8 * p
         c = [lanes_of(a[p], s + j) for j in range(8)]
-        pa, pe = a[p], e[p]
-        ra, re = pa, pe
+        pivot = a[p]
+        row = pivot
         for j in range(8):
             d = row_of(c[j], j)
             inv = 1.0 / d
             scale = lax.rsqrt(d)
             here = sub == j
             m = jnp.where(here, -inv, c[j] * inv)
-            qa, qe = row_of(pa, j), row_of(pe, j)
-            ra = jnp.where(here, qa * scale, ra)
-            re = jnp.where(here, qe * scale, re)
-            pa = jnp.where(here, 0.0, pa) - m * qa
-            pe = jnp.where(here, 0.0, pe) - m * qe
+            pivot = jnp.where(lane == s + j, jnp.where(here, 1.0, 0.0), pivot)
+            q = row_of(pivot, j)
+            row = jnp.where(here, q * scale, row)
+            pivot = jnp.where(here, 0.0, pivot) - m * q
             for k in range(j + 1, 8):
                 ck = row_of(c[k], j)
                 c[k] = jnp.where(here, 0.0, c[k]) - m * ck
-        upper.append(ra)
-        inverse.append(re)
-        qa = [row_of(pa, j) for j in range(8)]
-        qe = [row_of(pe, j) for j in range(8)]
-        for i in range(p + 1, tiles):
-            l = [lanes_of(a[i], s + j) for j in range(8)]
-            ua = [l[j] * qa[j] for j in range(8)]
-            ue = [l[j] * qe[j] for j in range(8)]
-            a[i] = a[i] - (((ua[0] + ua[1]) + (ua[2] + ua[3])) + ((ua[4] + ua[5]) + (ua[6] + ua[7])))
-            e[i] = e[i] - (((ue[0] + ue[1]) + (ue[2] + ue[3])) + ((ue[4] + ue[5]) + (ue[6] + ue[7])))
-    return upper, inverse
+        rows.append(row)
+        q = [row_of(pivot, j) for j in range(8)]
+        band = (lane >= s) & (lane < s + 8)
+        far = p + 1 + NEAR
+        if far < tiles:
+            left = jnp.concatenate([a[i][:, s : s + 8] for i in range(far, tiles)], axis=0)
+            prod = jnp.dot(left, pivot, precision=HI, preferred_element_type=F32)
+        for i in range(p + 1, min(far, tiles)):
+            u = [lanes_of(a[i], s + j) * q[j] for j in range(8)]
+            a[i] = jnp.where(band, 0.0, a[i]) - (((u[0] + u[1]) + (u[2] + u[3])) + ((u[4] + u[5]) + (u[6] + u[7])))
+        for i in range(far, tiles):
+            at = 8 * (i - far)
+            a[i] = jnp.where(band, 0.0, a[i]) - prod[at : at + 8, :]
+    return rows
 
 
 def chol_kernel(g_ref, w_hbm, modes_ref, r_ref, work, w_ref, first, second, stage, sem, w_sem):
@@ -447,11 +491,11 @@
     def _(kb):
         r0 = pl.multiple_of(kb * 128, 128)
         a = [work[pl.ds(pl.multiple_of(r0 + 8 * i, 8), 8), pl.ds(r0, 128)] for i in range(16)]
-        e = [jnp.where(lane == sub + 8 * i, 1.0, 0.0) for i in range(16)]
-        upper, inverse = factor_block(a, e)
-        for i in range(16):
-            work[pl.ds(pl.multiple_of(r0 + 8 * i, 8), 8), pl.ds(r0, 128)] = upper[i]
-            work[pl.ds(pl.multiple_of(r0 + 8 * i, 8), 8), pl.ds(pl.multiple_of(r0 + n, 128), 128)] = inverse[i]
+        for i, row in enumerate(factor_block(a)):
+            here = pl.ds(pl.multiple_of(r0 + 8 * i, 8), 8)
+            diagonal, left = lane == sub + 8 * i, lane <= sub + 8 * i
+            work[here, pl.ds(r0, 128)] = jnp.where(left, jnp.where(diagonal, 1.0 / row, 0.0), row)
+            work[here, pl.ds(pl.multiple_of(r0 + n, 128), 128)] = jnp.where(left, row, 0.0)
         own = pl.ds(r0, 128)
         linv = work[own, pl.ds(pl.multiple_of(r0 + n, 128), 128)]
         rest = pl.ds(pl.multiple_of(r0 + 128, 128), n - 128)
@@ -528,9 +572,7 @@
 
 
 def on_device(snapshots, lift, adjacency, codes, obstacle):
-    table = jnp.concatenate([adjacency, codes, obstacle[:, None]], axis=1)
-    table = jnp.pad(table, ((0, 0), (0, 128 - table.shape[1])))
-    weighted, gram = weigh_and_gram(snapshots, lift, table)
+    weighted, gram = weigh_and_gram(snapshots, lift, adjacency, codes, obstacle)
     return factor_and_modes(gram, weighted)
 
 

time: 121 us -> 115 us (0.950)
  Pallas kernels: 118 us -> 114 us
  local copies, waits for them, and re-layouts: 1.33 us -> 0 us
    pallas_call x1, Pallas kernels: 32.3 us -> 29.5 us  [factor_and_modes(): pl.pallas_call(chol_kernel, name='factor_modes', out_shape=(jax.ShapeDtyp...]
where the time goes in v3:
time: 115 us
  Pallas kernels  114 us (99%)
    pallas_call x1, Pallas kernels, weigh_and_gram(): pl.pallas_call(weigh_kernel, name='weigh_gram', out_shape=(jax.ShapeDtype...  84.5 us
    pallas_call x1, Pallas kernels, factor_and_modes(): pl.pallas_call(chol_kernel, name='factor_modes', out_shape=(jax.ShapeDtyp...  29.5 us

profile of v3, /device:TPU:1, one launch (start us, length us, event | category | flops | bytes accessed | tf_op | source)
XLA Modules:
  0.0 114.6 jit_solution(2901481812521114013)
XLA Ops:
  0.6 84.5 %weigh_gram.1 = (bf16[4096,512]{1,0:T(8,128)(2,1)}, f32[1280,128]{1,0:T(8,128)}) custom-call(bf16[16384,128]{1,0:T(8,128)(2,1)} %snap_ref.1, bf16[512,384]{1,0:T(8,128)(2,1)} %lift_hbm.1, s32[8,6]{1,0:T(8,128)} %adjacency_ref.1, s32[8,6]{1,0:T(8,128)} %codes_ref.1, s32[8]{0:T(128)} %obstacle_ref.1), custom_call_target="tpu_custom_call" | custom-call | tf_op jit(solution)/shard_map/weigh_gram/pallas_call | solution.py:403
  85.1 29.5 %factor_modes.1 = (f32[4096,512]{1,0:T(8,128)}, f32[512,512]{1,0:T(8,128)}) custom-call(f32[1280,128]{1,0:T(8,128)} %get-tuple-element.4.g_ref, bf16[4096,512]{1,0:T(8,128)(2,1)} %get-tuple-element.5.w_hbm), custom_call_target="tpu_custom_call" | custom-call | tf_op jit(solution)/shard_map/factor_modes/pallas_call | solution.py:556

commit v4 on v3

--- a/solution.py
+++ b/solution.py
@@ -1,3 +1,5 @@
+import functools
+
 import jax
 import jax.numpy as jnp
 from jax import lax
@@ -431,122 +433,176 @@
     return jnp.broadcast_to(x[row : row + 1, :], x.shape)
 
 
-def factor_block(a):
-    tiles = len(a)
+def tree_sum(terms):
+    while len(terms) > 1:
+        terms = [terms[i] + terms[i + 1] for i in range(0, len(terms), 2)]
+    return terms[0]
+
+
+def eliminate(c, pivot, s, follow=None):
     sub = lax.broadcasted_iota(jnp.int32, (8, 128), 0)
     lane = lax.broadcasted_iota(jnp.int32, (8, 128), 1)
+    row = pivot
+    if follow:
+        l, c2, nxt = follow
+    for j in range(8):
+        d = row_of(c[j], j)
+        inv = 1.0 / d
+        scale = lax.rsqrt(d)
+        here, unit = sub == j, lane == s + j
+        m = jnp.where(here, -inv, c[j] * inv)
+        pivot = jnp.where(unit, jnp.where(here, 1.0, 0.0), pivot)
+        q = row_of(pivot, j)
+        row = jnp.where(here, q * scale, row)
+        pivot = jnp.where(here, 0.0, pivot) - m * q
+        heads = {k: row_of(c[k], j) for k in range(j + 1, 8)}
+        for k in range(j + 1, 8):
+            c[k] = jnp.where(here, 0.0, c[k]) - m * heads[k]
+        if follow:
+            ml = l[j] * inv
+            nxt = jnp.where(unit, 0.0, nxt) - ml * q
+            for k in range(8):
+                c2[k] = c2[k] - ml * row_of(l[j], k)
+            for k in range(j + 1, 8):
+                l[k] = l[k] - ml * heads[k]
+    return pivot, row, nxt if follow else None
+
+
+def factor_block(a, beside):
+    tiles = len(a)
+    lane = lax.broadcasted_iota(jnp.int32, (8, 128), 1)
     rows = []
-    for p in range(tiles):
+    for p in range(0, tiles, 2):
         s = 8 * p
         c = [lanes_of(a[p], s + j) for j in range(8)]
-        pivot = a[p]
-        row = pivot
-        for j in range(8):
-            d = row_of(c[j], j)
-            inv = 1.0 / d
-            scale = lax.rsqrt(d)
-            here = sub == j
-            m = jnp.where(here, -inv, c[j] * inv)
-            pivot = jnp.where(lane == s + j, jnp.where(here, 1.0, 0.0), pivot)
-            q = row_of(pivot, j)
-            row = jnp.where(here, q * scale, row)
-            pivot = jnp.where(here, 0.0, pivot) - m * q
-            for k in range(j + 1, 8):
-                ck = row_of(c[k], j)
-                c[k] = jnp.where(here, 0.0, c[k]) - m * ck
+        l = [lanes_of(a[p + 1], s + j) for j in range(8)]
+        c2 = [lanes_of(a[p + 1], s + 8 + j) for j in range(8)]
+        far = p + 2 + NEAR
+        near = range(p + 2, min(far, tiles))
+        old = {i: [lanes_of(a[i], s + j) for j in range(16)] for i in near}
+        q1, row, nxt = eliminate(c, a[p], s, (l, c2, a[p + 1]))
         rows.append(row)
-        q = [row_of(pivot, j) for j in range(8)]
-        band = (lane >= s) & (lane < s + 8)
-        far = p + 1 + NEAR
+        beside(p)
+        u = [lanes_of(q1, s + 8 + j) for j in range(8)]
+        q2, row, _ = eliminate(c2, nxt, s + 8)
+        rows.append(row)
+        beside(p + 1)
+        if p + 2 == tiles:
+            break
+        heads = [row_of(q2, j) for j in range(8)]
+        q1 = jnp.where((lane >= s + 8) & (lane < s + 16), 0.0, q1) - tree_sum([u[j] * heads[j] for j in range(8)])
+        band = (lane >= s) & (lane < s + 16)
         if far < tiles:
-            left = jnp.concatenate([a[i][:, s : s + 8] for i in range(far, tiles)], axis=0)
-            prod = jnp.dot(left, pivot, precision=HI, preferred_element_type=F32)
-        for i in range(p + 1, min(far, tiles)):
-            u = [lanes_of(a[i], s + j) * q[j] for j in range(8)]
-            a[i] = jnp.where(band, 0.0, a[i]) - (((u[0] + u[1]) + (u[2] + u[3])) + ((u[4] + u[5]) + (u[6] + u[7])))
+            left = jnp.concatenate([a[i][:, s : s + 16] for i in range(far, tiles)], axis=0)
+            prod = jnp.dot(left, jnp.concatenate([q1, q2], axis=0), precision=HI, preferred_element_type=F32)
+        heads = [row_of(q1, j) for j in range(8)] + heads
+        for i in near:
+            a[i] = jnp.where(band, 0.0, a[i]) - tree_sum([old[i][j] * heads[j] for j in range(16)])
         for i in range(far, tiles):
             at = 8 * (i - far)
             a[i] = jnp.where(band, 0.0, a[i]) - prod[at : at + 8, :]
     return rows
 
 
-def chol_kernel(g_ref, w_hbm, modes_ref, r_ref, work, w_ref, first, second, stage, sem, w_sem):
-    n = r_ref.shape[0]
+def chol_kernel(g_ref, w_hbm, modes_ref, r_ref, work, w_ref, inv, stage, r_rows, sem, w_sem, r_sem, last_sem):
+    n = r_ref.shape[1]
     blocks = n // 128
     rows = w_ref.shape[0]
-    chunk = stage.shape[1]
-    half = n // 2
+    piece = rows // 16
     bring = pltpu.make_async_copy(w_hbm, w_ref, w_sem)
     bring.start()
-    work[...] = jnp.zeros_like(work)
-    index = 0
-    for bi in range(blocks):
-        for bj in range(bi, blocks):
-            work[bi * 128 : bi * 128 + 128, bj * 128 : bj * 128 + 128] = g_ref[index * 128 : index * 128 + 128, :]
-            index += 1
     sub = lax.broadcasted_iota(jnp.int32, (8, 128), 0)
     lane = lax.broadcasted_iota(jnp.int32, (8, 128), 1)
-
-    @pl.loop(0, blocks)
-    def _(kb):
-        r0 = pl.multiple_of(kb * 128, 128)
-        a = [work[pl.ds(pl.multiple_of(r0 + 8 * i, 8), 8), pl.ds(r0, 128)] for i in range(16)]
-        for i, row in enumerate(factor_block(a)):
-            here = pl.ds(pl.multiple_of(r0 + 8 * i, 8), 8)
+    NT = (((1,), (1,)), ((), ()))
+    order = [(i, j) for i in range(blocks) for j in range(i, blocks)]
+
+    def cols(j, count=1):
+        return pl.ds(j * 128, count * 128)
+
+    for index, (i, j) in enumerate(order):
+        work[cols(i), cols(j)] = g_ref[cols(index), :]
+    for i in range(1, blocks):
+        work[cols(i), cols(blocks, i)] = jnp.zeros((128, i * 128), F32)
+
+    def update(kb, i):
+        window = pl.ds(i * 128, n + (kb + 1 - i) * 128)
+        left = work[cols(kb), cols(i)].T
+        work[cols(i), window] = work[cols(i), window] - jnp.dot(
+            left, work[cols(kb), window], precision=HI, preferred_element_type=F32
+        )
+
+    def product(kb, first, count):
+        depth = (kb + 1) * 128
+        x = w_ref[pl.ds(first, count), 0:depth]
+        both = lax.dot_general(x, inv[kb % 2, :, 0:depth], NT, preferred_element_type=F32)
+        stage[kb % 2, pl.ds(first, count), :] = both[:, 0:128] + both[:, 128:256]
+
+    def out_copy(kb):
+        return pltpu.make_async_copy(stage.at[kb % 2], modes_ref.at[:, cols(kb)], sem.at[kb % 2])
+
+    def r_copy(kb):
+        return pltpu.make_async_copy(r_rows.at[cols(kb), :], r_ref.at[cols(kb), :], r_sem.at[kb])
+
+    for kb in range(blocks):
+        waiting = []
+        if kb >= 1:
+            waiting = [functools.partial(update, kb - 1, i) for i in range(kb + 1, blocks)]
+
+        def beside(p):
+            if waiting:
+                waiting.pop(0)()
+            if kb >= 1:
+                product(kb - 1, p * piece, piece)
+
+        if kb == 1:
+            bring.wait()
+        if kb >= 3:
+            out_copy(kb - 3).wait()
+        a = [work[pl.ds(kb * 128 + 8 * i, 8), cols(kb)] for i in range(16)]
+        for i, row in enumerate(factor_block(a, beside)):
+            here = pl.ds(kb * 128 + 8 * i, 8)
             diagonal, left = lane == sub + 8 * i, lane <= sub + 8 * i
-            work[here, pl.ds(r0, 128)] = jnp.where(left, jnp.where(diagonal, 1.0 / row, 0.0), row)
-            work[here, pl.ds(pl.multiple_of(r0 + n, 128), 128)] = jnp.where(left, row, 0.0)
-        own = pl.ds(r0, 128)
-        linv = work[own, pl.ds(pl.multiple_of(r0 + n, 128), 128)]
-        rest = pl.ds(pl.multiple_of(r0 + 128, 128), n - 128)
-        work[own, rest] = jnp.dot(linv, work[own, rest], precision=HI, preferred_element_type=F32)
-
-        @pl.loop(kb + 1, blocks)
-        def _(i):
-            ri = pl.multiple_of(i * 128, 128)
-            left = work[own, pl.ds(ri, 128)].T
-            window = pl.ds(pl.multiple_of(r0 + 128, 128), n)
-            work[pl.ds(ri, 128), window] = work[pl.ds(ri, 128), window] - jnp.dot(
-                left, work[own, window], precision=HI, preferred_element_type=F32
-            )
-
-    for part, r0, depth in ((first, 0, half), (second, half, n)):
-        row = work[r0 : r0 + half, n : n + depth]
+            r_rows[here, cols(kb)] = jnp.where(left, jnp.where(diagonal, 1.0 / row, 0.0), row)
+            work[here, cols(kb + blocks)] = jnp.where(left, row, 0.0)
+        if kb >= 1:
+            out_copy(kb - 1).start()
+        rest = pl.ds((kb + 1) * 128, n - 128)
+        work[cols(kb), rest] = jnp.dot(
+            work[cols(kb), cols(kb + blocks)], work[cols(kb), rest], precision=HI, preferred_element_type=F32
+        )
+        if kb + 1 < blocks:
+            update(kb, kb + 1)
+        depth = (kb + 1) * 128
+        row = work[cols(kb), pl.ds(n, depth)]
         high = row.astype(BF)
-        part[:, 0:depth] = high
-        part[:, depth : 2 * depth] = (row - high.astype(F32)).astype(BF)
-    bring.wait()
-    NT = (((1,), (1,)), ((), ()))
-
-    def out_copy(q):
-        slot = lax.rem(q, 2)
-        return pltpu.make_async_copy(
-            stage.at[slot], modes_ref.at[pl.ds(pl.multiple_of(q * chunk, chunk), chunk), :], sem.at[slot]
-        )
-
-    @pl.loop(0, rows // chunk)
+        inv[kb % 2, 0:128, 0:depth] = high
+        inv[kb % 2, 128:256, 0:depth] = (row - high.astype(F32)).astype(BF)
+        if kb > 0:
+            r_rows[cols(kb), cols(0, kb)] = jnp.zeros((128, kb * 128), F32)
+        if kb + 1 < blocks:
+            r_rows[cols(kb), cols(kb + 1, blocks - kb - 1)] = work[cols(kb), cols(kb + 1, blocks - kb - 1)]
+        r_copy(kb).start()
+
+    kb = blocks - 1
+    out_copy(kb - 2).wait()
+    chunk = rows // 8
+
+    def last_copy(q):
+        part = pl.ds(pl.multiple_of(q * chunk, chunk), chunk)
+        return pltpu.make_async_copy(stage.at[kb % 2, part, :], modes_ref.at[part, cols(kb)], last_sem.at[q])
+
+    @pl.loop(0, 8)
     def _(q):
-        slot = lax.rem(q, 2)
-
-        @pl.when(q >= 2)
-        def _():
-            out_copy(q - 2).wait()
-
-        x = w_ref[pl.ds(pl.multiple_of(q * chunk, chunk), chunk), :]
-        near = x[:, 0:half]
-        stage[slot, :, 0:half] = lax.dot_general(
-            jnp.concatenate([near, near], axis=1), first[...], NT, preferred_element_type=F32
-        )
-        stage[slot, :, half:n] = lax.dot_general(
-            jnp.concatenate([x, x], axis=1), second[...], NT, preferred_element_type=F32
-        )
-        out_copy(q).start()
-
-    out_copy(rows // chunk - 2).wait()
-    out_copy(rows // chunk - 1).wait()
-    ri = lax.broadcasted_iota(jnp.int32, (n, n), 0)
-    ci = lax.broadcasted_iota(jnp.int32, (n, n), 1)
-    r_ref[...] = jnp.where(ri <= ci, work[:, 0:n], 0.0)
+        product(kb, pl.multiple_of(q * chunk, chunk), chunk)
+        last_copy(q).start()
+
+    @pl.loop(0, 8)
+    def _(q):
+        last_copy(q).wait()
+
+    out_copy(kb - 1).wait()
+    for i in range(blocks):
+        r_copy(i).wait()
 
 
 def factor_and_modes(gram, weighted):
@@ -558,15 +614,17 @@
         name="factor_modes",
         out_shape=(jax.ShapeDtypeStruct((rows, n), F32), jax.ShapeDtypeStruct((n, n), F32)),
         in_specs=[vm, anyspace],
-        out_specs=(anyspace, vm),
+        out_specs=(anyspace, anyspace),
         scratch_shapes=[
             pltpu.VMEM((n, 2 * n), F32),
             pltpu.VMEM((rows, n), BF),
-            pltpu.VMEM((n // 2, n), BF),
-            pltpu.VMEM((n // 2, 2 * n), BF),
-            pltpu.VMEM((2, 512, n), F32),
+            pltpu.VMEM((2, 256, n), BF),
+            pltpu.VMEM((2, rows, 128), F32),
+            pltpu.VMEM((n, n), F32),
             pltpu.SemaphoreType.DMA((2,)),
             pltpu.SemaphoreType.DMA(()),
+            pltpu.SemaphoreType.DMA((n // 128,)),
+            pltpu.SemaphoreType.DMA((8,)),
         ],
     )(gram, weighted)
 

time: 115 us -> 105 us (0.913)
  Pallas kernels: 114 us -> 104 us
    pallas_call x1, Pallas kernels: 29.5 us -> 19.9 us  [factor_and_modes(): pl.pallas_call(chol_kernel, name='factor_modes', out_shape=(jax.ShapeDtyp...]
where the time goes in v4:
time: 105 us
  Pallas kernels  104 us (99%)
    pallas_call x1, Pallas kernels, weigh_and_gram(): pl.pallas_call(weigh_kernel, name='weigh_gram', out_shape=(jax.ShapeDtype...  84.5 us
    pallas_call x1, Pallas kernels, factor_and_modes(): pl.pallas_call(chol_kernel, name='factor_modes', out_shape=(jax.ShapeDtyp...  19.9 us

profile of v4, /device:TPU:1, one launch (start us, length us, event | category | flops | bytes accessed | tf_op | source)
XLA Modules:
  0.0 105.0 jit_solution(9357112064577942649)
XLA Ops:
  0.6 84.5 %weigh_gram.1 = (bf16[4096,512]{1,0:T(8,128)(2,1)}, f32[1280,128]{1,0:T(8,128)}) custom-call(bf16[16384,128]{1,0:T(8,128)(2,1)} %snap_ref.1, bf16[512,384]{1,0:T(8,128)(2,1)} %lift_hbm.1, s32[8,6]{1,0:T(8,128)} %adjacency_ref.1, s32[8,6]{1,0:T(8,128)} %codes_ref.1, s32[8]{0:T(128)} %obstacle_ref.1), custom_call_target="tpu_custom_call" | custom-call | tf_op jit(solution)/shard_map/weigh_gram/pallas_call | solution.py:405
  85.1 19.9 %factor_modes.1 = (f32[4096,512]{1,0:T(8,128)}, f32[512,512]{1,0:T(8,128)}) custom-call(f32[1280,128]{1,0:T(8,128)} %get-tuple-element.4.g_ref, bf16[4096,512]{1,0:T(8,128)(2,1)} %get-tuple-element.5.w_hbm), custom_call_target="tpu_custom_call" | custom-call | tf_op jit(solution)/shard_map/factor_modes/pallas_call | solution.py:612
